TPU v7x, 32 devices: a whole 2x2x4 slice. The times are simulated.
32 devices in a mesh: frame: 8 (over z, core), tok: 4 (over y, x).
Axes of the slice: x: 2, y: 2, z: 4, core: 2. Of those that a mesh axis runs over, the one named last changes fastest.
Arguments:
- stream: bfloat16 [8, 1024, 1152], P('frame', 'tok'), may hold values from -20 to 20
- queries: bfloat16 [8, 1024, 1152], P('frame', 'tok'), may hold values from -200 to 200
- key_vectors: bfloat16 [8, 1024, 1152], P('frame', 'tok'), may hold values from -6 to 6
- value_vectors: bfloat16 [8, 1024, 1152], P('frame', 'tok'), may hold values from -6 to 6
- modulation: float32 [8, 4, 1152], P('frame'), may hold values from -4 to 4
- output_weight: bfloat16 [1152, 1152], replicated, may hold values from -0.1875 to 0.1875
- output_bias: float32 [1152], replicated, may hold values from -3 to 3
- router_weight: bfloat16 [1152, 8], replicated, may hold values from -0.1875 to 0.1875
- expand_weight: bfloat16 [8, 1152, 4608], P('frame', None, 'tok'), may hold values from -0.1875 to 0.1875
- expand_bias: float32 [8, 4608], P('frame', 'tok'), may hold values from -3 to 3
- reduce_weight: bfloat16 [8, 4608, 1152], P('frame', 'tok'), may hold values from -0.09375 to 0.09375
- reduce_bias: float32 [8, 1152], P('frame'), may hold values from -3 to 3
- counts: int32 [8, 8], P(None, 'frame'), may hold values from 1 to 96, 256 in all within a row
- picked_rows: int32 [8, 8, 96], P(None, 'frame'), may hold values from 0 to 1023, as said below
Outputs:
- layer_out: bfloat16 [8, 1024, 1152], P('frame', 'tok')
Inputs may be any that keep to these rules, and one draw needn't show every extreme that they name: counts[e, g] slots of block (e, g) are used; the counts of one expert sum to 256. The entries of one block picked_rows[e, g, :] are distinct positions among the 1024 tokens of frame g; slots at or beyond counts[e, g] are unused.
All inputs are finite; a program needn't handle non-finite values.
Results may differ from a plain program's by a relative error of at most 0.0055.
Values may be sent and summed in bfloat16 or wider, within the bound.
A program may use at most 64 MiB of HBM per device.

v0:
```python
import math

import jax
import jax.numpy as jnp
from jax import lax
from jax.sharding import PartitionSpec as P

H = 16
HD = 72


def layer_norm(values):
    mean_val = jnp.mean(values, axis=-1, keepdims=True)
    centred = values - mean_val
    variance = jnp.mean(centred * centred, axis=-1, keepdims=True)
    return centred * lax.rsqrt(variance + 1e-06)


def head_attention(operands):
    head_queries, head_keys, head_values = operands
    length = head_queries.shape[1]
    block_rows = min(512, length)
    score_scale = 1.0 / math.sqrt(HD)

    def one_block(first_row):
        query_block = lax.dynamic_slice_in_dim(head_queries, first_row, block_rows, 1)
        scores = (
            lax.dot_general(
                query_block, head_keys, (((0,), (0,)), ((), ())), preferred_element_type=jnp.float32
            )
            * score_scale
        )
        scores = scores - jnp.max(scores, axis=1, keepdims=True)
        exponent = jnp.exp(scores)
        weights = (exponent / jnp.sum(exponent, axis=1, keepdims=True)).astype(jnp.bfloat16)
        return lax.dot_general(
            head_values, weights, (((1,), (1,)), ((), ())), preferred_element_type=jnp.float32
        ).astype(jnp.bfloat16)

    starts = jnp.arange(length // block_rows, dtype=jnp.int32) * block_rows
    blocks = lax.map(one_block, starts)
    return blocks.transpose(1, 0, 2).reshape(head_queries.shape[0], length)


def attend_items(pieces):
    outputs = lax.map(head_attention, (pieces[0][0], pieces[1][0], pieces[2][0]))
    return outputs[None]


def per_device(
    stream,
    queries,
    key_vectors,
    value_vectors,
    modulation,
    output_weight,
    output_bias,
    router_weight,
    expand_weight,
    expand_bias,
    reduce_weight,
    reduce_bias,
    counts,
    picked_rows,
):
    tok_groups = lax.axis_size("tok")
    tok_local = stream.shape[1]
    model_width = stream.shape[2]
    heads_local = H // tok_groups

    def to_heads(tensor):
        return tensor[0].reshape(tok_local, tok_groups, heads_local, HD).transpose(1, 2, 3, 0)

    attended = attend_items(
        (
            lax.all_to_all(to_heads(queries), "tok", split_axis=0, concat_axis=3, tiled=True),
            lax.all_to_all(to_heads(key_vectors), "tok", split_axis=0, concat_axis=3, tiled=True),
            lax.all_to_all(to_heads(value_vectors), "tok", split_axis=0, concat_axis=3, tiled=True),
        )
    )
    returned = lax.all_to_all(attended, "tok", split_axis=3, concat_axis=0, tiled=True)
    attended_rows = returned.transpose(3, 0, 1, 2).reshape(tok_local, model_width)
    projected = (
        jnp.dot(attended_rows, output_weight, preferred_element_type=jnp.float32) + output_bias
    )
    shares = modulation[0]
    residual = (stream[0].astype(jnp.float32) + shares[0] * projected).astype(jnp.bfloat16)
    normed = (layer_norm(residual.astype(jnp.float32)) * (1.0 + shares[2]) + shares[1]).astype(
        jnp.bfloat16
    )
    gate_values = jax.nn.sigmoid(jnp.dot(normed, router_weight, preferred_element_type=jnp.float32))
    slot_count = picked_rows.shape[2]
    local_pos = picked_rows[:, 0, :] - lax.axis_index("tok") * tok_local
    in_use = jnp.arange(slot_count, dtype=jnp.int32)[None, :] < counts
    on_shard = in_use & (local_pos >= 0) & (local_pos < tok_local)
    safe_pos = jnp.clip(local_pos, 0, tok_local - 1)
    chosen = jnp.take(normed, safe_pos, axis=0)
    chosen = jnp.where(on_shard[:, :, None], chosen, jnp.zeros_like(chosen))
    moved = lax.all_to_all(chosen, "frame", split_axis=0, concat_axis=1, tiled=True)
    expert_rows = lax.psum(moved.astype(jnp.float32).astype(jnp.bfloat16), "tok")
    hidden = jax.nn.gelu(
        jnp.einsum("erd,edf->erf", expert_rows, expand_weight, preferred_element_type=jnp.float32)
        + expand_bias[:, None, :],
        approximate=True,
    ).astype(jnp.bfloat16)
    partial_out = jnp.einsum(
        "erf,efd->erd", hidden, reduce_weight, preferred_element_type=jnp.float32
    )
    column_count = model_width // tok_groups
    summed = lax.psum_scatter(
        partial_out.astype(jnp.bfloat16), "tok", scatter_dimension=2, tiled=True
    ).astype(jnp.float32)
    bias_part = lax.dynamic_slice_in_dim(
        reduce_bias, lax.axis_index("tok") * column_count, column_count, 1
    )
    expert_out = (summed + bias_part[:, None, :]).astype(jnp.bfloat16)
    returned_cols = lax.all_to_all(expert_out, "frame", split_axis=1, concat_axis=0, tiled=True)
    returned_rows = lax.all_gather(returned_cols, "tok", axis=2, tiled=True)
    mix_weight = jnp.take_along_axis(gate_values.T, safe_pos, axis=1)
    mix_weight = jnp.where(on_shard, mix_weight, jnp.zeros_like(mix_weight)).astype(jnp.bfloat16)
    targets = jnp.arange(tok_local, dtype=jnp.int32)
    matches = (safe_pos.reshape(-1)[None, :] == targets[:, None]) & on_shard.reshape(-1)[None, :]
    scatter_table = jnp.where(matches, mix_weight.reshape(-1)[None, :], jnp.zeros((), jnp.bfloat16))
    expert_mix = jnp.dot(
        scatter_table, returned_rows.reshape(-1, model_width), preferred_element_type=jnp.float32
    )
    layer_out = (residual.astype(jnp.float32) + shares[3] * expert_mix).astype(jnp.bfloat16)
    return layer_out[None]


def solution(mesh):
    return jax.shard_map(
        per_device,
        mesh=mesh,
        in_specs=(
            P("frame", "tok", None),
            P("frame", "tok", None),
            P("frame", "tok", None),
            P("frame", "tok", None),
            P("frame", None, None),
            P(),
            P(),
            P(),
            P("frame", None, "tok"),
            P("frame", "tok"),
            P("frame", "tok", None),
            P("frame", None),
            P(None, "frame"),
            P(None, "frame", None),
        ),
        out_specs=P("frame", "tok", None),
        check_vma=False,
    )
```

profile of v0, /device:TPU:25, one launch (start us, length us, event | category | flops | bytes accessed | tf_op | source)
XLA Modules:
  0.0 380.9 jit_solution(11425842389973880382)
XLA Ops:
  14.4 5.9 %all-to-all-done = bf16[4,4,72,256]{3,2,1,0:T(8,128)(2,1)S(1)} async-done(((bf16[4,4,72,256]{3,2,1,0:T(8,128)(2,1)}), bf16[4,4,72,256]{3,2,1,0:T(8,128)(2,1)S(1)}, u32[]{:S(2)}, u32[]{:S(2)}) %all-to-all-start) | async-done | bytes 589856 | tf_op jit(solution)/shard_map/all_to_all | solution.py:76
  20.3 4.3 %all-to-all-start.1 = ((bf16[4,4,72,256]{3,2,1,0:T(8,128)(2,1)}), bf16[4,4,72,256]{3,2,1,0:T(8,128)(2,1)}, u32[]{:S(2)}, u32[]{:S(2)}) async-start(bf16[4,4,72,256]{3,2,1,0:T(8,128)(2,1)} %bitcast.127), calls=%async_computation.1 | async-start | bytes 1179648 | tf_op jit(solution)/shard_map/all_to_all | solution.py:77
  26.8 5.3 %all-to-all-done.1 = bf16[4,4,72,256]{3,2,1,0:T(8,128)(2,1)} async-done(((bf16[4,4,72,256]{3,2,1,0:T(8,128)(2,1)}), bf16[4,4,72,256]{3,2,1,0:T(8,128)(2,1)}, u32[]{:S(2)}, u32[]{:S(2)}) %all-to-all-start.1) | async-done | bytes 589856 | tf_op jit(solution)/shard_map/all_to_all | solution.py:77
  32.1 4.2 %all-to-all-start.2 = ((bf16[4,4,72,256]{3,2,1,0:T(8,128)(2,1)}), bf16[4,4,72,256]{3,2,1,0:T(8,128)(2,1)}, u32[]{:S(2)}, u32[]{:S(2)}) async-start(bf16[4,4,72,256]{3,2,1,0:T(8,128)(2,1)} %bitcast.126), calls=%async_computation.2 | async-start | bytes 1179648 | tf_op jit(solution)/shard_map/all_to_all | solution.py:78
  45.7 45.9 %while.21 = (s32[]{:T(128)}, bf16[4,72,1024]{2,1,0:T(8,128)(2,1)}, bf16[4,72,1024]{2,1,0:T(8,128)(2,1)}, bf16[4,72,1024]{2,1,0:T(8,128)(2,1)}, bf16[4,72,1024]{2...) while((s32[]{:T(128)}, bf16[4,72,1024]{2,1,0:T(8,128)(2,1)}, ...), condition=%wide.region_5.6_spmd, body=%wide.region_0.5_spmd.sunk | while | flops 155749376 | bytes 8513900 | solution.py:46
  47.7 8.6 %while.22 = (s32[]{:T(128)}, bf16[2,72,512]{2,1,0:T(8,128)(2,1)S(1)}, s32[2]{0:T(128)S(1)}, bf16[72,1024]{1,0:T(8,128)(2,1)S(1)}, bf16[72,1024]{1,0:T(8,128)(2,1...) while((s32[]{:T(128)}, bf16[2,72,512]{2,1,0:T(8,128)(2,1)S(1)}, ...), condition=%wide.region_4.4_spmd, body=%wide.region_1.3_spmd.sunk | while | flops 155749376 | bytes 6744219 | solution.py:41
  59.2 8.6 %while.22 = (s32[]{:T(128)}, bf16[2,72,512]{2,1,0:T(8,128)(2,1)S(1)}, s32[2]{0:T(128)S(1)}, bf16[72,1024]{1,0:T(8,128)(2,1)S(1)}, bf16[72,1024]{1,0:T(8,128)(2,1...) while((s32[]{:T(128)}, bf16[2,72,512]{2,1,0:T(8,128)(2,1)S(1)}, ...), condition=%wide.region_4.4_spmd, body=%wide.region_1.3_spmd.sunk | while | flops 155749376 | bytes 6744219 | solution.py:41
  70.7 8.6 %while.22 = (s32[]{:T(128)}, bf16[2,72,512]{2,1,0:T(8,128)(2,1)S(1)}, s32[2]{0:T(128)S(1)}, bf16[72,1024]{1,0:T(8,128)(2,1)S(1)}, bf16[72,1024]{1,0:T(8,128)(2,1...) while((s32[]{:T(128)}, bf16[2,72,512]{2,1,0:T(8,128)(2,1)S(1)}, ...), condition=%wide.region_4.4_spmd, body=%wide.region_1.3_spmd.sunk | while | flops 155749376 | bytes 6744219 | solution.py:41
  82.2 8.6 %while.22 = (s32[]{:T(128)}, bf16[2,72,512]{2,1,0:T(8,128)(2,1)S(1)}, s32[2]{0:T(128)S(1)}, bf16[72,1024]{1,0:T(8,128)(2,1)S(1)}, bf16[72,1024]{1,0:T(8,128)(2,1...) while((s32[]{:T(128)}, bf16[2,72,512]{2,1,0:T(8,128)(2,1)S(1)}, ...), condition=%wide.region_4.4_spmd, body=%wide.region_1.3_spmd.sunk | while | flops 155749376 | bytes 6744219 | solution.py:41
  94.0 4.4 %all-to-all-start.3 = ((bf16[1,4,72,1024]{2,1,0,3:T(4,128)(2,1)}), bf16[1,4,72,1024]{2,1,0,3:T(4,128)(2,1)}, u32[]{:S(2)}, u32[]{:S(2)}) async-start(bf16[1,4,72,1024]{2,1,0,3:T(4,128)(2,1)} %bitcast.123), calls=%async_computation.3 | async-start | bytes 2097152 | tf_op jit(solution)/shard_map/all_to_all | solution.py:81
  98.6 13.1 %all-to-all-done.3 = bf16[1,4,72,1024]{2,1,0,3:T(4,128)(2,1)} async-done(((bf16[1,4,72,1024]{2,1,0,3:T(4,128)(2,1)}), bf16[1,4,72,1024]{2,1,0,3:T(4,128)(2,1)}, u32[]{:S(2)}, u32[]{:S(2)}) %all-to-all-start.3) | async-done | bytes 589856 | tf_op jit(solution)/shard_map/all_to_all | solution.py:81
  123.0 45.5 %all_to_all.87 = bf16[8,96,1152]{2,1,0:T(8,128)(2,1)} all-to-all(bf16[8,96,1152]{2,1,0:T(8,128)(2,1)S(1)} %select_select_fusion), channel_id=1, replica_groups=mesh['frame'=8,'tok'=4] {'frame'}, dimensions={0} | all-to-all | bytes 3538944 | tf_op jit(solution)/shard_map/all_to_all | solution.py:99
  169.2 63.1 %all-reduce.2.cloned.1.call-done = bf16[768,1152]{1,0:T(8,128)(2,1)} async-done(((bf16[768,1152]{1,0:T(8,128)(2,1)}), bf16[768,1152]{1,0:T(8,128)(2,1)}) %all-reduce.2.cloned.1.call-update) | async-done | bytes 1769488 | tf_op jit(solution)/shard_map/psum | solution.py:100
  232.3 8.8 %fusion.15 = bf16[1,768,1152]{2,1,0:T(8,128)(2,1)} fusion(bf16[1,1152,1152]{2,1,0:T(8,128)(2,1)S(1)} %copy-done, bf16[768,1152]{1,0:T(8,128)(2,1)} %all-reduce.2.cloned.1.call-done, bf16[1,1152,1152]{2,1,0:T(8,128)(2,1)} %param.26, f32[1152]{0:T(1024)S(1)} %reduce.5), kind=kOutput, calls=%fused_computation.29 | convolution fusion | flops 4086595584 | bytes 8851968 | tf_op jit(solution)/shard_map/erf,efd->erd/dot_general | solution.py:106
  241.1 8.8 %copy.95 = bf16[1,768,1152]{1,0,2:T(2,128)(2,1)} copy(bf16[1,768,1152]{2,1,0:T(8,128)(2,1)} %fusion.15) | data formatting | bytes 3538944
  254.3 31.8 %reduce-scatter.4.cloned.1.call-done = bf16[288,768]{1,0:T(8,128)(2,1)} async-done(((bf16[1152,768]{1,0:T(8,128)(2,1)}), bf16[288,768]{1,0:T(8,128)(2,1)}) %reduce-scatter.4.cloned.1.call-update) | async-done | bytes 442384
  288.4 4.6 %copy.90 = bf16[1,768,288]{2,0,1:T(2,128)(2,1)} copy(bf16[1,768,288]{1,2,0:T(8,128)(2,1)} %add_convert_fusion.1) | data formatting | bytes 884736 | tf_op jit(solution)/shard_map/convert_element_type | solution.py:116
  293.6 6.1 %reduce.13 = bf16[768,288]{1,0:T(8,128)(2,1)} reduce(bf16[768,1,288]{2,1,0:T(2,128)(2,1)} %bitcast.121, bf16[]{:T(256)} %broadcast.265), dimensions={1}, to_apply=%bitcast.92.reduce_sub_computation | reduce | bytes 884738
  302.3 16.6 %all_to_all.88 = bf16[8,2,13824]{2,1,0:T(2,128)(2,1)} all-to-all(bf16[8,2,13824]{2,1,0:T(2,128)(2,1)} %reshape.249), channel_id=1, replica_groups=mesh['frame'=8,'tok'=4] {'frame'}, dimensions={0} | all-to-all | bytes 884736 | tf_op jit(solution)/shard_map/all_to_all | solution.py:117
  318.9 3.8 reshape.250
  322.7 4.5 %copy.91 = bf16[1,768,288]{1,2,0:T(8,128)(2,1)} copy(bf16[1,768,288]{2,0,1:T(2,128)(2,1)} %bitcast.122) | data formatting | bytes 884736 | tf_op jit(solution)/shard_map/all_to_all | solution.py:117
  330.4 6.5 %gather_fusion.1 = bf16[768]{0:T(1024)(128)(2,1)S(1)} fusion(bf16[8,256]{1,0:T(8,128)(2,1)S(1)} %fusion.28, s32[768]{0:T(1024)S(1)} %reshape.231), kind=kCustom, calls=%fused_computation.1 | custom fusion | bytes 9216 | tf_op jit(solution)/shard_map/jit(take_along_axis)/gather | solution.py:119
  336.9 30.0 %all-gather.2.cloned.1.call-done = bf16[8,96,1152]{1,0,2:T(8,128)(2,1)} async-done(((bf16[8,96,288]{1,0,2:T(8,128)(2,1)}), bf16[8,96,1152]{1,0,2:T(8,128)(2,1)}) %all-gather.2.cloned.1.call-update) | async-done | bytes 1769488 | tf_op jit(solution)/shard_map/all_gather | solution.py:118
  366.9 4.2 %copy.92 = bf16[8,96,1152]{2,1,0:T(8,128)(2,1)} copy(bf16[8,96,1152]{1,0,2:T(8,128)(2,1)} %all-gather.2.cloned.1.call-done) | data formatting | bytes 3538944 | tf_op jit(solution)/shard_map/all_gather | solution.py:118
  (127 shorter events, 81.3 us)
Async XLA Ops:
  6.5 225.8 %copy-start = (bf16[1,1152,1152]{2,1,0:T(8,128)(2,1)S(1)}, bf16[1,1152,1152]{2,1,0:T(8,128)(2,1)}, u32[]{:S(2)}) copy-start(bf16[1,1152,1152]{2,1,0:T(8,128)(2,1)} %param.28) | copy-start | bytes 7962628
  8.8 11.5 %all-to-all-start = ((bf16[4,4,72,256]{3,2,1,0:T(8,128)(2,1)}), bf16[4,4,72,256]{3,2,1,0:T(8,128)(2,1)S(1)}, u32[]{:S(2)}, u32[]{:S(2)}) async-start(bf16[4,4,72,256]{3,2,1,0:T(8,128)(2,1)} %bitcast.128), calls=%async_computation | async-start | bytes 1179648 | tf_op jit(solution)/shard_map/all_to_all | solution.py:76
  12.3 14.5 %copy-start.5 = (s32[8,1,96]{2,1,0:T(1,128)S(1)}, s32[8,1,96]{2,1,0:T(1,128)}, u32[]{:S(2)}) copy-start(s32[8,1,96]{2,1,0:T(1,128)} %param.31) | copy-start | bytes 9220
  20.3 16.0 %copy-start.3 = (f32[1,4,1152]{2,1,0:T(4,128)S(1)}, f32[1,4,1152]{2,1,0:T(4,128)}, u32[]{:S(2)}) copy-start(f32[1,4,1152]{2,1,0:T(4,128)} %param.22) | copy-start | bytes 55300
  20.3 11.8 %all-to-all-start.1 = ((bf16[4,4,72,256]{3,2,1,0:T(8,128)(2,1)}), bf16[4,4,72,256]{3,2,1,0:T(8,128)(2,1)}, u32[]{:S(2)}, u32[]{:S(2)}) async-start(bf16[4,4,72,256]{3,2,1,0:T(8,128)(2,1)} %bitcast.127), calls=%async_computation.1 | async-start | bytes 1179648 | tf_op jit(solution)/shard_map/all_to_all | solution.py:77
  32.1 10.8 %all-to-all-start.2 = ((bf16[4,4,72,256]{3,2,1,0:T(8,128)(2,1)}), bf16[4,4,72,256]{3,2,1,0:T(8,128)(2,1)}, u32[]{:S(2)}, u32[]{:S(2)}) async-start(bf16[4,4,72,256]{3,2,1,0:T(8,128)(2,1)} %bitcast.126), calls=%async_computation.2 | async-start | bytes 1179648 | tf_op jit(solution)/shard_map/all_to_all | solution.py:78
  91.7 6.8 %copy-start.6 = (s32[8,1]{0,1:T(1,128)S(1)}, s32[8,1]{0,1:T(1,128)}, u32[]{:S(2)}) copy-start(s32[8,1]{0,1:T(1,128)} %param.30) | copy-start | bytes 100
  94.0 19.1 %copy-start.7 = (f32[1152]{0:T(1024)S(1)}, f32[1152]{0:T(1024)}, u32[]{:S(2)}) copy-start(f32[1152]{0:T(1024)} %param.24) | copy-start | bytes 13828
  94.0 17.6 %all-to-all-start.3 = ((bf16[1,4,72,1024]{2,1,0,3:T(4,128)(2,1)}), bf16[1,4,72,1024]{2,1,0,3:T(4,128)(2,1)}, u32[]{:S(2)}, u32[]{:S(2)}) async-start(bf16[1,4,72,1024]{2,1,0,3:T(4,128)(2,1)} %bitcast.123), calls=%async_computation.3 | async-start | bytes 2097152 | tf_op jit(solution)/shard_map/all_to_all | solution.py:81
  98.4 133.9 %all-reduce.2.cloned.1.call-start = ((), (), s32[]{:S(2)}) async-start(), calls=%async_computation.7 | async-start | bytes 3538944 | tf_op jit(solution)/shard_map/psum | solution.py:100
  116.2 1.0 copy-start.1
  168.5 0.7 copy-start.4
  168.5 117.6 %reduce-scatter.4.cloned.1.call-start = ((), (), s32[]{:S(2)}) async-start(), calls=%async_computation.9 | async-start | bytes 2211840
  253.5 113.4 %all-gather.2.cloned.1.call-start = ((), (), s32[]{:S(2)}) async-start(), calls=%async_computation.8 | async-start | bytes 2949120 | tf_op jit(solution)/shard_map/all_gather | solution.py:118
  322.7 7.4 %copy-start.2 = (bf16[1152,8]{0,1:T(8,128)(2,1)S(1)}, bf16[1152,8]{0,1:T(8,128)(2,1)}, u32[]{:S(2)}) copy-start(bf16[1152,8]{0,1:T(8,128)(2,1)} %param.25) | copy-start | bytes 55300
Sparse Core Ops, SparseCore 0:
  168.6 63.6 all-reduce.1
  253.6 32.4 reduce-scatter.3
  329.8 36.9 all-gather.1
where the time goes:
time: 385 us; the launch traced here: 381 us
  waiting for transfers between devices  149 us (39%)
  local copies, waits for them, and re-layouts  84.8 us (22%)
  blocking collectives  62.1 us (16%)
  matrix products  25.9 us (7%)
  starting transfers between devices  16.6 us (4%)
  loops' own time  15 us (4%)
  other arithmetic  13.9 us (4%)
  between operations  13.3 us (3%)
    psum x1, waiting for transfers between devices, per_device(): lax.psum(moved.astype(jnp.float32).astype(jnp.bfloat16), 'tok')  63.1 us
    all_to_all x1, blocking collectives, per_device(): lax.all_to_all(chosen, 'frame', split_axis=0, concat_axis=1, tiled=True)  45.5 us
    unnamed x4, waiting for transfers between devices  31.8 us
    all_gather x1, waiting for transfers between devices, per_device(): returned_rows = lax.all_gather(returned_cols, 'tok', axis=2, tiled=True)  30 us
    unnamed x25, local copies, waits for them, and re-layouts  28.5 us
    all_to_all x1, blocking collectives, per_device(): lax.all_to_all(expert_out, 'frame', split_axis=1, concat_axis=0, tiled=True)  16.6 us
    another operation x4, loops' own time, head_attention(): blocks = lax.map(one_block, starts)  14.8 us
    all_to_all x1, waiting for transfers between devices, per_device(): lax.all_to_all(attended, 'tok', split_axis=3, concat_axis=0, tiled=True)  13.1 us
  transfers between devices with their start and end apart: 7, of which 7 were waited for; matrix products, arithmetic and copies ran while one was open for 5% of the time, Pallas kernels for 0%

commit v1 on v0

v1 whole, which is shorter than its diff:
```python
import functools
import math

import jax
import jax.numpy as jnp
from jax import lax
from jax.experimental import pallas as pl
from jax.experimental.pallas import tpu as pltpu
from jax.sharding import PartitionSpec as P

H = 16
HD = 72
CAP = 256
BF = jnp.bfloat16
F32 = jnp.float32


def dot(a, b, ca, cb):
    return lax.dot_general(a, b, (((ca,), (cb,)), ((), ())), preferred_element_type=F32)


def attention_kernel(q_ref, k_ref, v_ref, o_ref):
    sources = q_ref.shape[0]
    scale = math.log2(math.e) / math.sqrt(HD)
    keys = jnp.concatenate([k_ref[s, 0] for s in range(sources)], axis=1).T
    values = jnp.concatenate([v_ref[s, 0] for s in range(sources)], axis=1)

    def block(j, carry):
        scores = dot(keys, q_ref[j, 0], 1, 0)
        top = jnp.max(scores, axis=0, keepdims=True)
        powers = jnp.exp2((scores - top) * scale)
        total = jnp.sum(powers, axis=0, keepdims=True)
        out = dot(values, powers.astype(BF), 1, 0)
        o_ref[j, 0] = (out / total).astype(BF)
        return carry

    lax.fori_loop(0, sources, block, 0)


def attention(q, k, v):
    sources, heads, _, tokens = q.shape
    spec = pl.BlockSpec((sources, 1, HD, tokens), lambda h: (0, h, 0, 0))
    return pl.pallas_call(
        attention_kernel,
        out_shape=jax.ShapeDtypeStruct(q.shape, BF),
        grid=(heads,),
        in_specs=[spec] * 3,
        out_specs=spec,
        compiler_params=pltpu.CompilerParams(vmem_limit_bytes=48 << 20),
    )(q, k, v)


def swap(x, axis):
    return lax.all_to_all(x, axis, split_axis=0, concat_axis=0, tiled=True)


def per_device(
    stream,
    queries,
    key_vectors,
    value_vectors,
    modulation,
    output_weight,
    output_bias,
    router_weight,
    expand_weight,
    expand_bias,
    reduce_weight,
    reduce_bias,
    counts,
    picked_rows,
):
    shards = lax.axis_size("tok")
    tokens = stream.shape[1]
    width = stream.shape[2]
    cols = width // shards
    heads = H // shards
    experts, _, slots = picked_rows.shape
    frame_tokens = tokens * shards

    def to_heads(x):
        return swap(x[0].T.reshape(shards, heads, HD, tokens), "tok")

    attended = attention(to_heads(queries), to_heads(key_vectors), to_heads(value_vectors))
    attended = swap(attended, "tok").reshape(width, tokens)
    shares = modulation[0].T
    projected = dot(output_weight, attended, 0, 0) + output_bias[:, None]
    residual = (stream[0].T.astype(F32) + shares[:, 0:1] * projected).astype(BF)
    wide = residual.astype(F32)
    centred = wide - jnp.mean(wide, axis=0, keepdims=True)
    variance = jnp.mean(centred * centred, axis=0, keepdims=True)
    normed = (
        centred * lax.rsqrt(variance + 1e-06) * (1.0 + shares[:, 2:3]) + shares[:, 1:2]
    ).astype(BF)
    gates = jax.nn.sigmoid(dot(router_weight, normed, 0, 0)).astype(BF)
    sent = jnp.concatenate(
        [
            normed.reshape(shards, cols, tokens),
            jnp.broadcast_to(gates[None], (shards, experts, tokens)),
        ],
        axis=1,
    )
    held = swap(sent, "tok").transpose(1, 0, 2).reshape(cols + experts, frame_tokens)
    used = jnp.arange(slots, dtype=jnp.int32)[None, :] < counts
    where_to = jnp.where(used, picked_rows[:, 0, :], -1)
    hits = where_to[:, :, None] == jnp.arange(frame_tokens, dtype=jnp.int32)[None, None, :]
    pick = hits.astype(BF).reshape(experts * slots, frame_tokens)
    chosen = dot(pick, held[:cols], 1, 1).astype(BF)
    arrived = swap(chosen.reshape(experts, slots, cols), "frame").reshape(-1, cols)
    own_counts = swap(counts, "frame")[:, 0]
    first = jnp.cumsum(own_counts) - own_counts
    slot = jnp.arange(slots, dtype=jnp.int32)[None, :]
    row = jnp.where(slot < own_counts[:, None], first[:, None] + slot, -1).reshape(-1)
    pack = (jnp.arange(CAP, dtype=jnp.int32)[:, None] == row[None, :]).astype(BF)
    rows = dot(pack, arrived, 1, 0).astype(BF)
    all_rows = swap(jnp.broadcast_to(rows[None], (shards, CAP, cols)), "tok")
    all_rows = all_rows.transpose(1, 0, 2).reshape(CAP, width)
    hidden = jax.nn.gelu(
        dot(all_rows, expand_weight[0], 1, 0) + expand_bias, approximate=True
    ).astype(BF)
    partial_out = dot(hidden, reduce_weight[0], 1, 0).astype(BF)
    pieces = swap(partial_out.reshape(CAP, shards, cols).transpose(1, 0, 2), "tok")
    bias = lax.dynamic_slice_in_dim(reduce_bias, lax.axis_index("tok") * cols, cols, 1)
    expert_out = (jnp.sum(pieces.astype(F32), axis=0) + bias).astype(BF)
    spread = dot(pack, expert_out, 0, 0).astype(BF)
    returned = swap(spread.reshape(-1, slots, cols), "frame").reshape(-1, cols)
    table = jnp.where(hits, held[cols:][:, None, :], jnp.zeros((), BF))
    mixed = dot(returned, table.reshape(experts * slots, frame_tokens), 0, 0).astype(BF)
    mixed = swap(mixed.reshape(cols, shards, tokens).transpose(1, 0, 2), "tok")
    mixed = mixed.reshape(width, tokens).astype(F32)
    layer_out = (residual.astype(F32) + shares[:, 3:4] * mixed).astype(BF)
    return layer_out.T[None]


def solution(mesh):
    return jax.shard_map(
        per_device,
        mesh=mesh,
        in_specs=(
            P("frame", "tok", None),
            P("frame", "tok", None),
            P("frame", "tok", None),
            P("frame", "tok", None),
            P("frame", None, None),
            P(),
            P(),
            P(),
            P("frame", None, "tok"),
            P("frame", "tok"),
            P("frame", "tok", None),
            P("frame", None),
            P(None, "frame"),
            P(None, "frame", None),
        ),
        out_specs=P("frame", "tok", None),
        check_vma=False,
    )
```

time: 385 us -> 204 us (0.53)
  the two profiles are of different devices: /device:TPU:25 before, /device:TPU:0 now
where the time goes in v1:
time: 204 us; the launch traced here: 203 us
  waiting for transfers between devices  73.4 us (36%)
  starting transfers between devices  38.9 us (19%)
  local copies, waits for them, and re-layouts  30.5 us (15%)
  blocking collectives  23.3 us (11%)
  matrix products  14.2 us (7%)
  Pallas kernels  13.2 us (6%)
  other arithmetic  8.76 us (4%)
    all_to_all x9, waiting for transfers between devices, swap(): return lax.all_to_all(x, axis, split_axis=0, concat_axis=0, tiled=True)  73.4 us
    all_to_all x9, starting transfers between devices, swap(): return lax.all_to_all(x, axis, split_axis=0, concat_axis=0, tiled=True)  38.9 us
    all_to_all x2, blocking collectives, swap(): return lax.all_to_all(x, axis, split_axis=0, concat_axis=0, tiled=True)  23.3 us
    dot_general x7, matrix products, dot(): lax.dot_general(a, b, (((ca,), (cb,)), ((), ())), preferred_element_type=...  14.2 us
    pallas_call x1, Pallas kernels, attention(): pl.pallas_call(attention_kernel, out_shape=jax.ShapeDtypeStruct(q.shape,...  13.2 us
    transpose x3, local copies, waits for them, and re-layouts, to_heads(): return swap(x[0].T.reshape(shards, heads, HD, tokens), 'tok')  6.5 us
    reshape x2, local copies, waits for them, and re-layouts, per_device(): chosen.reshape(experts, slots, cols)  4.45 us
    reshape x2, local copies, waits for them, and re-layouts, per_device(): returned = swap(spread.reshape(-1, slots, cols), 'frame').reshape(-1, cols)  4.43 us
  transfers between devices with their start and end apart: 9, of which 8 were waited for; matrix products, arithmetic and copies ran while one was open for 7% of the time, Pallas kernels for 0%

profile of v1, /device:TPU:0, one launch (start us, length us, event | category | flops | bytes accessed | tf_op | source)
XLA Modules:
  0.0 202.6 jit_solution(15611413486651829619)
XLA Ops:
  2.3 5.2 %all-to-all-start = ((bf16[4,4,72,256]{3,2,1,0:T(8,128)(2,1)}), bf16[4,4,72,256]{3,2,1,0:T(8,128)(2,1)S(1)}, u32[]{:S(2)}, u32[]{:S(2)}) async-start(bf16[4,4,72,256]{3,2,1,0:T(8,128)(2,1)} %bitcast.100), calls=%async_computation | async-start | bytes 1179648 | tf_op jit(solution)/shard_map/all_to_all | solution.py:54
  9.6 6.6 %all-to-all-done.q_ref = bf16[4,4,72,256]{3,2,1,0:T(8,128)(2,1)S(1)} async-done(((bf16[4,4,72,256]{3,2,1,0:T(8,128)(2,1)}), bf16[4,4,72,256]{3,2,1,0:T(8,128)(2,1)S(1)}, u32[]{:S(2)}, u32[]{:S(2)}) %all-to-all-start) | async-done | bytes 589856 | tf_op jit(solution)/shard_map/all_to_all | solution.py:54
  16.2 4.1 %all-to-all-start.1 = ((bf16[4,4,72,256]{3,2,1,0:T(8,128)(2,1)}), bf16[4,4,72,256]{3,2,1,0:T(8,128)(2,1)}, u32[]{:S(2)}, u32[]{:S(2)}) async-start(bf16[4,4,72,256]{3,2,1,0:T(8,128)(2,1)} %bitcast.99), calls=%async_computation.1 | async-start | bytes 1179648 | tf_op jit(solution)/shard_map/all_to_all | solution.py:54
  22.5 6.0 %all-to-all-done.1.k_ref = bf16[4,4,72,256]{3,2,1,0:T(8,128)(2,1)} async-done(((bf16[4,4,72,256]{3,2,1,0:T(8,128)(2,1)}), bf16[4,4,72,256]{3,2,1,0:T(8,128)(2,1)}, u32[]{:S(2)}, u32[]{:S(2)}) %all-to-all-start.1) | async-done | bytes 589856 | tf_op jit(solution)/shard_map/all_to_all | solution.py:54
  28.5 11.6 %all_to_all.59.v_ref = bf16[4,4,72,256]{3,2,1,0:T(8,128)(2,1)S(1)} all-to-all(bf16[4,4,72,256]{3,2,1,0:T(8,128)(2,1)} %bitcast.101), channel_id=1, replica_groups=mesh['frame'=8,'tok'=4] {'tok'}, dimensions={0} | all-to-all | bytes 1179648 | tf_op jit(solution)/shard_map/all_to_all | solution.py:54
  40.0 13.2 %shard_map.136 = bf16[4,4,72,256]{3,2,1,0:T(8,128)(2,1)S(1)} custom-call(bf16[4,4,72,256]{3,2,1,0:T(8,128)(2,1)S(1)} %all-to-all-done.q_ref, bf16[4,4,72,256]{3,2,1,0:T(8,128)(2,1)} %all-to-all-done.1.k_ref, bf16[4,4,72,256]{3,2,1,0:T(8,128)(2,1)S(1)} %all_to_all.59.v_ref), custom_call_target="tpu_custom_call" | custom-call | tf_op jit(solution)/shard_map/pallas_call | solution.py:43
  54.1 3.6 %all-to-all-start.3 = ((bf16[4,4,72,256]{3,2,1,0:T(8,128)(2,1)}), bf16[4,4,72,256]{3,2,1,0:T(8,128)(2,1)S(1)}, u32[]{:S(2)}, u32[]{:S(2)}) async-start(bf16[4,4,72,256]{3,2,1,0:T(8,128)(2,1)} %copy-done.1), calls=%async_computation.3 | async-start | bytes 1179648 | tf_op jit(solution)/shard_map/all_to_all | solution.py:54
  57.8 6.9 %all-to-all-done.3 = bf16[4,4,72,256]{3,2,1,0:T(8,128)(2,1)S(1)} async-done(((bf16[4,4,72,256]{3,2,1,0:T(8,128)(2,1)}), bf16[4,4,72,256]{3,2,1,0:T(8,128)(2,1)S(1)}, u32[]{:S(2)}, u32[]{:S(2)}) %all-to-all-start.3) | async-done | bytes 589856 | tf_op jit(solution)/shard_map/all_to_all | solution.py:54
  71.5 3.5 %all-to-all-start.5 = ((bf16[4,296,256]{2,1,0:T(8,128)(2,1)}), bf16[4,296,256]{2,1,0:T(8,128)(2,1)S(1)}, u32[]{:S(2)}, u32[]{:S(2)}) async-start(bf16[4,296,256]{2,1,0:T(8,128)(2,1)} %pad_maximum_fusion), calls=%async_computation.5 | async-start | bytes 1212416 | tf_op jit(solution)/shard_map/all_to_all | solution.py:54
  77.1 4.9 %all-to-all-done.5 = bf16[4,296,256]{2,1,0:T(8,128)(2,1)S(1)} async-done(((bf16[4,296,256]{2,1,0:T(8,128)(2,1)}), bf16[4,296,256]{2,1,0:T(8,128)(2,1)S(1)}, u32[]{:S(2)}, u32[]{:S(2)}) %all-to-all-start.5) | async-done | bytes 606240 | tf_op jit(solution)/shard_map/all_to_all | solution.py:54
  82.0 4.9 %all-to-all-start.4 = ((s32[8,1,1]{2,1,0:T(1,128)}), s32[8,1,1]{2,1,0:T(1,128)S(1)}, u32[]{:S(2)}, u32[]{:S(2)}) async-start(s32[8,1,1]{2,1,0:T(1,128)} %copy.45), calls=%async_computation.4 | async-start | bytes 8192 | tf_op jit(solution)/shard_map/all_to_all | solution.py:54
  88.7 2.5 %reshape.163 = bf16[8,96,288]{1,0,2:T(8,128)(2,1)} reshape(bf16[768,288]{0,1:T(8,128)(2,1)} %fusion.22) | data formatting | bytes 884736 | tf_op jit(solution)/shard_map/reshape | solution.py:109
  93.1 5.1 %all-to-all-start.6 = ((bf16[8,96,288]{1,2,0:T(8,128)(2,1)}), bf16[8,96,288]{1,2,0:T(8,128)(2,1)}, u32[]{:S(2)}, u32[]{:S(2)}) async-start(bf16[8,96,288]{1,2,0:T(8,128)(2,1)} %copy.48), calls=%async_computation.6 | async-start | bytes 1179648 | tf_op jit(solution)/shard_map/all_to_all | solution.py:54
  98.8 16.3 %all-to-all-done.6 = bf16[8,96,288]{1,2,0:T(8,128)(2,1)} async-done(((bf16[8,96,288]{1,2,0:T(8,128)(2,1)}), bf16[8,96,288]{1,2,0:T(8,128)(2,1)}, u32[]{:S(2)}, u32[]{:S(2)}) %all-to-all-start.6) | async-done | bytes 442400 | tf_op jit(solution)/shard_map/all_to_all | solution.py:54
  121.7 4.2 %all-to-all-start.7 = ((bf16[4,256,288]{1,2,0:T(8,128)(2,1)}), bf16[4,256,288]{1,2,0:T(8,128)(2,1)}, u32[]{:S(2)}, u32[]{:S(2)}) async-start(bf16[4,256,288]{1,2,0:T(8,128)(2,1)} %broadcast_in_dim.49), calls=%async_computation.7 | async-start | bytes 1179648 | tf_op jit(solution)/shard_map/all_to_all | solution.py:54
  125.9 8.7 %all-to-all-done.7 = bf16[4,256,288]{1,2,0:T(8,128)(2,1)} async-done(((bf16[4,256,288]{1,2,0:T(8,128)(2,1)}), bf16[4,256,288]{1,2,0:T(8,128)(2,1)}, u32[]{:S(2)}, u32[]{:S(2)}) %all-to-all-start.7) | async-done | bytes 589856 | tf_op jit(solution)/shard_map/all_to_all | solution.py:54
  134.7 5.7 %fusion.7 = bf16[256,1152]{1,0:T(8,128)(2,1)} fusion(bf16[1,1152,1152]{2,1,0:T(8,128)(2,1)} %param.24, bf16[256,1152]{0,1:T(8,128)(2,1)} %bitcast.22, bf16[1,1152,1152]{2,1,0:T(8,128)(2,1)} %param.22, f32[1152]{0:T(1024)S(1)} %reduce.8), kind=kOutput, calls=%fused_computation.11 | convolution fusion | flops 1362198528 | bytes 6492672 | tf_op jit(solution)/shard_map/dot_general | solution.py:19
  142.5 4.2 %all-to-all-start.8 = ((bf16[4,256,288]{1,2,0:T(8,128)(2,1)}), bf16[4,256,288]{1,2,0:T(8,128)(2,1)}, u32[]{:S(2)}, u32[]{:S(2)}) async-start(bf16[4,256,288]{1,2,0:T(8,128)(2,1)} %bitcast.98), calls=%async_computation.8 | async-start | bytes 1179648 | tf_op jit(solution)/shard_map/all_to_all | solution.py:54
  147.4 7.3 %all-to-all-done.8 = bf16[4,256,288]{1,2,0:T(8,128)(2,1)} async-done(((bf16[4,256,288]{1,2,0:T(8,128)(2,1)}), bf16[4,256,288]{1,2,0:T(8,128)(2,1)}, u32[]{:S(2)}, u32[]{:S(2)}) %all-to-all-start.8) | async-done | bytes 589856 | tf_op jit(solution)/shard_map/all_to_all | solution.py:54
  161.5 4.2 %all-to-all-start.9 = ((bf16[8,96,288]{1,2,0:T(8,128)(2,1)}), bf16[8,96,288]{1,2,0:T(8,128)(2,1)}, u32[]{:S(2)}, u32[]{:S(2)}) async-start(bf16[8,96,288]{1,2,0:T(8,128)(2,1)} %copy.51), calls=%async_computation.9 | async-start | bytes 1179648 | tf_op jit(solution)/shard_map/all_to_all | solution.py:54
  165.8 16.7 %all-to-all-done.9 = bf16[8,96,288]{1,2,0:T(8,128)(2,1)} async-done(((bf16[8,96,288]{1,2,0:T(8,128)(2,1)}), bf16[8,96,288]{1,2,0:T(8,128)(2,1)}, u32[]{:S(2)}, u32[]{:S(2)}) %all-to-all-start.9) | async-done | bytes 442400 | tf_op jit(solution)/shard_map/all_to_all | solution.py:54
  184.4 11.8 %all_to_all.60 = bf16[4,288,256]{2,1,0:T(8,128)(2,1)S(1)} all-to-all(bf16[4,288,256]{2,1,0:T(8,128)(2,1)S(1)} %bitcast.103), channel_id=1, replica_groups=mesh['frame'=8,'tok'=4] {'tok'}, dimensions={0} | all-to-all | bytes 1179648 | tf_op jit(solution)/shard_map/all_to_all | solution.py:54
  197.3 2.7 %copy.53 = f32[1152,256]{0,1:T(8,128)} copy(f32[1152,256]{1,0:T(8,128)} %bitcast_convert_fusion) | data formatting | bytes 2359296 | tf_op jit(solution)/shard_map/convert_element_type | solution.py:130
  200.0 2.6 %fusion.45 = bf16[1,256,1152]{2,1,0:T(8,128)(2,1)} fusion(f32[1152,256]{0,1:T(8,128)} %copy.53, f32[256,1152]{1,0:T(8,128)} %copy-done.2, f32[1152]{0:T(1024)S(1)} %get-tuple-element.5), kind=kLoop, calls=%fused_computation.47 | loop fusion | flops 884736 | bytes 2953728 | tf_op jit(solution)/shard_map/broadcast_in_dim | solution.py:132
  (64 shorter events, 40.0 us)
Async XLA Ops:
  0.0 64.6 %copy-start = (bf16[1152,1152]{1,0:T(8,128)(2,1)S(1)}, bf16[1152,1152]{1,0:T(8,128)(2,1)}, u32[]{:S(2)}) copy-start(bf16[1152,1152]{1,0:T(8,128)(2,1)} %param.19) | copy-start | bytes 7962628
  2.3 13.9 %all-to-all-start = ((bf16[4,4,72,256]{3,2,1,0:T(8,128)(2,1)}), bf16[4,4,72,256]{3,2,1,0:T(8,128)(2,1)S(1)}, u32[]{:S(2)}, u32[]{:S(2)}) async-start(bf16[4,4,72,256]{3,2,1,0:T(8,128)(2,1)} %bitcast.100), calls=%async_computation | async-start | bytes 1179648 | tf_op jit(solution)/shard_map/all_to_all | solution.py:54
  16.2 12.3 %all-to-all-start.1 = ((bf16[4,4,72,256]{3,2,1,0:T(8,128)(2,1)}), bf16[4,4,72,256]{3,2,1,0:T(8,128)(2,1)}, u32[]{:S(2)}, u32[]{:S(2)}) async-start(bf16[4,4,72,256]{3,2,1,0:T(8,128)(2,1)} %bitcast.99), calls=%async_computation.1 | async-start | bytes 1179648 | tf_op jit(solution)/shard_map/all_to_all | solution.py:54
  53.2 0.8 copy-start.1
  54.1 3.6 %copy-start.4 = (f32[1,4,1152]{2,1,0:T(4,128)S(1)}, f32[1,4,1152]{2,1,0:T(4,128)}, u32[]{:S(2)}) copy-start(f32[1,4,1152]{2,1,0:T(4,128)} %param.18) | copy-start | bytes 55300
  54.1 10.6 %copy-start.8 = (f32[1152]{0:T(1024)S(1)}, f32[1152]{0:T(1024)}, u32[]{:S(2)}) copy-start(f32[1152]{0:T(1024)} %param.20) | copy-start | bytes 13828
  54.1 10.6 %all-to-all-start.3 = ((bf16[4,4,72,256]{3,2,1,0:T(8,128)(2,1)}), bf16[4,4,72,256]{3,2,1,0:T(8,128)(2,1)S(1)}, u32[]{:S(2)}, u32[]{:S(2)}) async-start(bf16[4,4,72,256]{3,2,1,0:T(8,128)(2,1)} %copy-done.1), calls=%async_computation.3 | async-start | bytes 1179648 | tf_op jit(solution)/shard_map/all_to_all | solution.py:54
  66.9 1.0 copy-start.2
  67.9 1.3 copy-start.3
  69.5 5.5 %copy-start.7 = (s32[8,1]{0,1:T(1,128)S(1)}, s32[8,1]{0,1:T(1,128)}, u32[]{:S(2)}) copy-start(s32[8,1]{0,1:T(1,128)} %param.26) | copy-start | bytes 100
  69.5 6.2 %copy-start.5 = (s32[8,1,96]{2,1,0:T(1,128)S(1)}, s32[8,1,96]{2,1,0:T(1,128)}, u32[]{:S(2)}) copy-start(s32[8,1,96]{2,1,0:T(1,128)} %param.27) | copy-start | bytes 9220
  71.5 10.5 %all-to-all-start.5 = ((bf16[4,296,256]{2,1,0:T(8,128)(2,1)}), bf16[4,296,256]{2,1,0:T(8,128)(2,1)S(1)}, u32[]{:S(2)}, u32[]{:S(2)}) async-start(bf16[4,296,256]{2,1,0:T(8,128)(2,1)} %pad_maximum_fusion), calls=%async_computation.5 | async-start | bytes 1212416 | tf_op jit(solution)/shard_map/all_to_all | solution.py:54
  82.0 11.1 %all-to-all-start.4 = ((s32[8,1,1]{2,1,0:T(1,128)}), s32[8,1,1]{2,1,0:T(1,128)S(1)}, u32[]{:S(2)}, u32[]{:S(2)}) async-start(s32[8,1,1]{2,1,0:T(1,128)} %copy.45), calls=%async_computation.4 | async-start | bytes 8192 | tf_op jit(solution)/shard_map/all_to_all | solution.py:54
  93.1 21.9 %all-to-all-start.6 = ((bf16[8,96,288]{1,2,0:T(8,128)(2,1)}), bf16[8,96,288]{1,2,0:T(8,128)(2,1)}, u32[]{:S(2)}, u32[]{:S(2)}) async-start(bf16[8,96,288]{1,2,0:T(8,128)(2,1)} %copy.48), calls=%async_computation.6 | async-start | bytes 1179648 | tf_op jit(solution)/shard_map/all_to_all | solution.py:54
  119.5 6.4 %copy-start.6 = (f32[1,1152]{1,0:T(1,128)S(1)}, f32[1,1152]{1,0:T(1,128)}, u32[]{:S(2)}) copy-start(f32[1,1152]{1,0:T(1,128)} %param.23) | copy-start | bytes 13828
  121.7 12.9 %all-to-all-start.7 = ((bf16[4,256,288]{1,2,0:T(8,128)(2,1)}), bf16[4,256,288]{1,2,0:T(8,128)(2,1)}, u32[]{:S(2)}, u32[]{:S(2)}) async-start(bf16[4,256,288]{1,2,0:T(8,128)(2,1)} %broadcast_in_dim.49), calls=%async_computation.7 | async-start | bytes 1179648 | tf_op jit(solution)/shard_map/all_to_all | solution.py:54
  142.5 12.3 %all-to-all-start.8 = ((bf16[4,256,288]{1,2,0:T(8,128)(2,1)}), bf16[4,256,288]{1,2,0:T(8,128)(2,1)}, u32[]{:S(2)}, u32[]{:S(2)}) async-start(bf16[4,256,288]{1,2,0:T(8,128)(2,1)} %bitcast.98), calls=%async_computation.8 | async-start | bytes 1179648 | tf_op jit(solution)/shard_map/all_to_all | solution.py:54
  161.5 20.9 %all-to-all-start.9 = ((bf16[8,96,288]{1,2,0:T(8,128)(2,1)}), bf16[8,96,288]{1,2,0:T(8,128)(2,1)}, u32[]{:S(2)}, u32[]{:S(2)}) async-start(bf16[8,96,288]{1,2,0:T(8,128)(2,1)} %copy.51), calls=%async_computation.9 | async-start | bytes 1179648 | tf_op jit(solution)/shard_map/all_to_all | solution.py:54

commit v2 on v1

v2 whole, which is shorter than its diff:
```python
import functools
import math

import jax
import jax.numpy as jnp
from jax import lax
from jax.experimental import pallas as pl
from jax.experimental.pallas import tpu as pltpu
from jax.sharding import PartitionSpec as P

H = 16
HD = 72
CAP = 256
BF = jnp.bfloat16
F32 = jnp.float32


def dot(a, b, ca, cb):
    return lax.dot_general(a, b, (((ca,), (cb,)), ((), ())), preferred_element_type=F32)


def attention_kernel(q_ref, k_ref, v_ref, o_ref):
    sources = q_ref.shape[0]
    scale = math.log2(math.e) / math.sqrt(HD)
    keys = jnp.concatenate([k_ref[s, 0] for s in range(sources)], axis=1).T
    values = jnp.concatenate([v_ref[s, 0] for s in range(sources)], axis=1)

    def block(j, carry):
        scores = dot(keys, q_ref[j, 0], 1, 0)
        top = jnp.max(scores, axis=0, keepdims=True)
        powers = jnp.exp2((scores - top) * scale)
        total = jnp.sum(powers, axis=0, keepdims=True)
        out = dot(values, powers.astype(BF), 1, 0)
        o_ref[j, 0] = (out / total).astype(BF)
        return carry

    lax.fori_loop(0, sources, block, 0)


def attention(q, k, v):
    sources, heads, _, tokens = q.shape
    spec = pl.BlockSpec((sources, 1, HD, tokens), lambda h: (0, h, 0, 0))
    return pl.pallas_call(
        attention_kernel,
        out_shape=jax.ShapeDtypeStruct(q.shape, BF),
        grid=(heads,),
        in_specs=[spec] * 3,
        out_specs=spec,
        compiler_params=pltpu.CompilerParams(vmem_limit_bytes=48 << 20),
    )(q, k, v)


def swap(x, axis):
    return lax.all_to_all(x, axis, split_axis=0, concat_axis=0, tiled=True)


MESH = pl.DeviceIdType.MESH


def gelu(x):
    return 0.5 * x * (1.0 + jnp.tanh(math.sqrt(2.0 / math.pi) * (x + 0.044715 * (x * x * x))))


def tail_kernel(
    att_ref,
    stream_ref,
    mod_ref,
    out_bias_ref,
    router_ref,
    expand_bias_ref,
    reduce_bias_ref,
    counts_ref,
    where_ref,
    wo_hbm,
    we_hbm,
    wr_hbm,
    o_ref,
    wo,
    we,
    wr,
    att_in,
    normed_out,
    normed_in,
    gate_out,
    gate_in,
    count_in,
    chosen_out,
    chosen_in,
    rows_all,
    part_out,
    part_in,
    ret_out,
    ret_in,
    mix_out,
    mix_in,
    local_sem,
    tok_send,
    tok_recv,
    frame_send,
    frame_recv,
):
    shards, cols, tokens = att_in.shape
    frames, slots = chosen_in.shape[0], chosen_in.shape[1]
    experts = gate_in.shape[1]
    frame_tokens = shards * tokens
    size = {"tok": shards, "frame": frames}
    me = {"tok": lax.axis_index("tok"), "frame": lax.axis_index("frame")}
    sems = {"tok": (tok_send, tok_recv), "frame": (frame_send, frame_recv)}

    loads = [
        pltpu.make_async_copy(src, dst, local_sem.at[i])
        for i, (src, dst) in enumerate(((wo_hbm, wo), (we_hbm, we), (wr_hbm, wr)))
    ]
    for load in loads:
        load.start()

    barrier = pltpu.get_barrier_semaphore()
    for axis in ("tok", "frame"):
        for d in range(1, size[axis]):
            p = lax.rem(me[axis] + d, size[axis])
            pl.semaphore_signal(barrier, inc=1, device_id={axis: p}, device_id_type=MESH)
    pl.semaphore_wait(barrier, shards + frames - 2)

    def copy(axis, phase, src, dst, to, slot):
        send, recv = sems[axis]
        return pltpu.make_async_remote_copy(
            src_ref=src,
            dst_ref=dst.at[slot],
            send_sem=send.at[phase, to],
            recv_sem=recv.at[phase, slot],
            device_id={axis: to},
            device_id_type=MESH,
        )

    sent = []

    def send_to(axis, phase, source, dst, d):
        p = lax.rem(me[axis] + d, size[axis])
        made = copy(axis, phase, source(p), dst, p, me[axis])
        made.start()
        sent.append(made)

    def send_all(axis, phase, source, dst):
        for d in range(1, size[axis]):
            send_to(axis, phase, source, dst, d)

    def take(axis, phase, source, dst, d):
        q = lax.rem(me[axis] + size[axis] - d, size[axis])
        copy(axis, phase, source(q), dst, q, q).wait_recv()
        return q

    def take_all(axis, phase, source, dst):
        for d in range(1, size[axis]):
            take(axis, phase, source, dst, d)

    tok, frame = me["tok"], me["frame"]
    send_all("tok", 0, lambda p: att_ref.at[p], att_in)
    send_all("frame", 0, lambda p: counts_ref.at[p], count_in)
    att_in[tok] = att_ref[tok]
    count_in[frame] = counts_ref[frame]
    loads[0].wait()
    take_all("tok", 0, lambda p: att_ref.at[p], att_in)

    projected = dot(att_in[0].T, wo[0:cols, :], 1, 0)
    for s in range(1, shards):
        projected += dot(att_in[s].T, wo[s * cols : (s + 1) * cols, :], 1, 0)
    projected += out_bias_ref[...]
    residual = (stream_ref[...].astype(F32) + mod_ref[0:1] * projected).astype(BF)
    wide = residual.astype(F32)
    centred = wide - jnp.mean(wide, axis=1, keepdims=True)
    variance = jnp.mean(centred * centred, axis=1, keepdims=True)
    normed = (
        centred * lax.rsqrt(variance + 1e-06) * (1.0 + mod_ref[2:3]) + mod_ref[1:2]
    ).astype(BF)
    turned = normed.T
    for s in range(shards):
        normed_out[s] = turned[s * cols : (s + 1) * cols]
    send_all("tok", 1, lambda p: normed_out.at[p], normed_in)
    o_ref[...] = residual
    gates = dot(router_ref[...], normed, 1, 1)
    gate_out[...] = 1.0 / (1.0 + jnp.exp(-gates))
    send_all("tok", 2, lambda p: gate_out, gate_in)
    normed_in[tok] = normed_out[tok]
    gate_in[tok] = gate_out[...]

    token = lax.broadcasted_iota(jnp.int32, (slots, frame_tokens), 1)

    def hits(e):
        return where_ref[e] == token

    take_all("frame", 0, lambda p: counts_ref.at[p], count_in)
    row = lax.broadcasted_iota(jnp.int32, (CAP, slots), 0)
    slot = lax.broadcasted_iota(jnp.int32, (CAP, slots), 1)
    first = jnp.zeros((1, slots), jnp.int32)
    firsts, numbers = [], []
    for g in range(frames):
        number = count_in[g][0:1, 0:slots]
        firsts.append(first)
        numbers.append(number)
        first = first + number

    def pack(g):
        return jnp.where((row == firsts[g] + slot) & (slot < numbers[g]), 1.0, 0.0)

    take_all("tok", 1, lambda p: normed_out.at[p], normed_in)
    held = jnp.concatenate([normed_in[s] for s in range(shards)], axis=1)
    for e in range(experts):
        pick = jnp.where(hits(e), 1.0, 0.0).astype(BF)
        chosen_out[e] = dot(pick, held, 1, 1).astype(BF)
    send_all("frame", 1, lambda p: chosen_out.at[p], chosen_in)
    chosen_in[frame] = chosen_out[frame]
    take_all("frame", 1, lambda p: chosen_out.at[p], chosen_in)
    rows = dot(pack(0).astype(BF), chosen_in[0], 1, 0)
    for g in range(1, frames):
        rows += dot(pack(g).astype(BF), chosen_in[g], 1, 0)
    rows_all[tok] = rows.astype(BF)
    send_all("tok", 3, lambda p: rows_all.at[tok], rows_all)
    loads[1].wait()
    loads[2].wait()
    take_all("tok", 3, lambda p: rows_all.at[tok], rows_all)
    hidden = dot(rows_all[0], we[0:cols, :], 1, 0)
    for s in range(1, shards):
        hidden += dot(rows_all[s], we[s * cols : (s + 1) * cols, :], 1, 0)
    hidden = gelu(hidden + expand_bias_ref[...]).astype(BF)
    partial_out = dot(hidden, wr[...], 1, 0)
    for s in range(shards):
        part_out[s] = partial_out[:, s * cols : (s + 1) * cols].astype(BF)
    send_all("tok", 4, lambda p: part_out.at[p], part_in)
    part_in[tok] = part_out[tok]
    take_all("tok", 4, lambda p: part_out.at[p], part_in)
    total = part_in[0].astype(F32)
    for s in range(1, shards):
        total += part_in[s].astype(F32)
    expert_out = (total + reduce_bias_ref[tok]).astype(BF)
    for g in range(frames):
        ret_out[g] = dot(pack(g).T.astype(BF), expert_out, 1, 0).astype(BF)
    send_all("frame", 2, lambda p: ret_out.at[p], ret_in)
    ret_in[frame] = ret_out[frame]
    take_all("tok", 2, lambda p: gate_out, gate_in)
    gate_all = jnp.concatenate([gate_in[s] for s in range(shards)], axis=1)
    take_all("frame", 2, lambda p: ret_out.at[p], ret_in)
    mixed = jnp.zeros((cols, frame_tokens), F32)
    for e in range(experts):
        table = jnp.where(hits(e), gate_all[e : e + 1], 0.0).astype(BF)
        mixed += dot(ret_in[e].T, table, 1, 0)
    for s in range(shards):
        mix_out[s] = mixed[:, s * tokens : (s + 1) * tokens].astype(BF)
    send_all("tok", 5, lambda p: mix_out.at[p], mix_in)
    mix_in[tok] = mix_out[tok]
    take_all("tok", 5, lambda p: mix_out.at[p], mix_in)
    mix = jnp.concatenate([mix_in[s].astype(F32) for s in range(shards)], axis=0).T
    o_ref[...] = (o_ref[...].astype(F32) + mod_ref[3:4] * mix).astype(BF)
    for made in sent:
        made.wait_send()


def per_device(
    stream,
    queries,
    key_vectors,
    value_vectors,
    modulation,
    output_weight,
    output_bias,
    router_weight,
    expand_weight,
    expand_bias,
    reduce_weight,
    reduce_bias,
    counts,
    picked_rows,
):
    shards = lax.axis_size("tok")
    frames = lax.axis_size("frame")
    tokens = stream.shape[1]
    width = stream.shape[2]
    hidden = expand_weight.shape[2]
    cols = width // shards
    heads = H // shards
    experts, _, slots = picked_rows.shape

    def to_heads(x):
        return swap(x[0].T.reshape(shards, heads, HD, tokens), "tok")

    attended = attention(to_heads(queries), to_heads(key_vectors), to_heads(value_vectors))
    attended = attended.reshape(shards, cols, tokens)
    used = jnp.arange(slots, dtype=jnp.int32)[None, :] < counts
    where_to = jnp.where(used, picked_rows[:, 0, :], -1)[:, :, None]
    vmem = pl.BlockSpec(memory_space=pltpu.VMEM)
    hbm = pl.BlockSpec(memory_space=pl.ANY)
    layer_out = pl.pallas_call(
        tail_kernel,
        out_shape=jax.ShapeDtypeStruct((tokens, width), BF),
        in_specs=[vmem] * 9 + [hbm] * 3,
        out_specs=vmem,
        scratch_shapes=[
            pltpu.VMEM((width, width), BF),
            pltpu.VMEM((width, hidden), BF),
            pltpu.VMEM((hidden, width), BF),
            pltpu.VMEM((shards, cols, tokens), BF),
            pltpu.VMEM((shards, cols, tokens), BF),
            pltpu.VMEM((shards, cols, tokens), BF),
            pltpu.VMEM((experts, tokens), F32),
            pltpu.VMEM((shards, experts, tokens), F32),
            pltpu.VMEM((frames, 8, 128), jnp.int32),
            pltpu.VMEM((frames, slots, cols), BF),
            pltpu.VMEM((frames, slots, cols), BF),
            pltpu.VMEM((shards, CAP, cols), BF),
            pltpu.VMEM((shards, CAP, cols), BF),
            pltpu.VMEM((shards, CAP, cols), BF),
            pltpu.VMEM((frames, slots, cols), BF),
            pltpu.VMEM((frames, slots, cols), BF),
            pltpu.VMEM((shards, cols, tokens), BF),
            pltpu.VMEM((shards, cols, tokens), BF),
            pltpu.SemaphoreType.DMA((3,)),
            pltpu.SemaphoreType.DMA((6, shards)),
            pltpu.SemaphoreType.DMA((6, shards)),
            pltpu.SemaphoreType.DMA((3, frames)),
            pltpu.SemaphoreType.DMA((3, frames)),
        ],
        compiler_params=pltpu.CompilerParams(
            collective_id=1, has_side_effects=True, vmem_limit_bytes=56 << 20
        ),
    )(
        attended,
        stream[0],
        modulation[0],
        output_bias[None],
        router_weight.T,
        expand_bias,
        reduce_bias.reshape(shards, 1, cols),
        jnp.broadcast_to(counts[:, :, None], (experts, 8, 128)),
        where_to,
        output_weight,
        expand_weight[0],
        reduce_weight[0],
    )
    return layer_out[None]


def solution(mesh):
    return jax.shard_map(
        per_device,
        mesh=mesh,
        in_specs=(
            P("frame", "tok", None),
            P("frame", "tok", None),
            P("frame", "tok", None),
            P("frame", "tok", None),
            P("frame", None, None),
            P(),
            P(),
            P(),
            P("frame", None, "tok"),
            P("frame", "tok"),
            P("frame", "tok", None),
            P("frame", None),
            P(None, "frame"),
            P(None, "frame", None),
        ),
        out_specs=P("frame", "tok", None),
        check_vma=False,
    )
```

time: 204 us -> 143 us (0.70)
  the two profiles are of different devices: /device:TPU:0 before, /device:TPU:25 now
where the time goes in v2:
time: 143 us; the launch traced here: 142 us
  Pallas kernels  104 us (73%)
  waiting for transfers between devices  17.5 us (12%)
  starting transfers between devices  10.4 us (7%)
  local copies, waits for them, and re-layouts  9.25 us (6%)
    pallas_call x1, Pallas kernels, per_device(): pl.pallas_call(tail_kernel, out_shape=jax.ShapeDtypeStruct((tokens, width...  91.6 us
    all_to_all x3, waiting for transfers between devices, swap(): return lax.all_to_all(x, axis, split_axis=0, concat_axis=0, tiled=True)  17.5 us
    pallas_call x1, Pallas kernels, attention(): pl.pallas_call(attention_kernel, out_shape=jax.ShapeDtypeStruct(q.shape,...  12.4 us
    all_to_all x3, starting transfers between devices, swap(): return lax.all_to_all(x, axis, split_axis=0, concat_axis=0, tiled=True)  10.4 us
    transpose x3, local copies, waits for them, and re-layouts, to_heads(): return swap(x[0].T.reshape(shards, heads, HD, tokens), 'tok')  4.34 us
  transfers between devices with their start and end apart: 3, of which 3 were waited for; matrix products, arithmetic and copies ran while one was open for 3% of the time, Pallas kernels for 0%

profile of v2, /device:TPU:25, one launch (start us, length us, event | category | flops | bytes accessed | tf_op | source)
XLA Modules:
  0.0 142.1 jit_solution(7890325243041923512)
XLA Ops:
  0.0 2.2 %copy.18 = bf16[1152,256]{1,0:T(8,128)(2,1)} copy(bf16[1152,256]{0,1:T(8,128)(2,1)} %bitcast.26) | data formatting | bytes 1179648 | tf_op jit(solution)/shard_map/transpose | solution.py:283
  2.2 3.5 %all-to-all-start = ((bf16[4,4,72,256]{3,2,1,0:T(8,128)(2,1)}), bf16[4,4,72,256]{3,2,1,0:T(8,128)(2,1)S(1)}, u32[]{:S(2)}, u32[]{:S(2)}) async-start(bf16[4,4,72,256]{3,2,1,0:T(8,128)(2,1)} %bitcast.2), calls=%async_computation | async-start | bytes 1179648 | tf_op jit(solution)/shard_map/all_to_all | solution.py:54
  5.7 0.0 copy-start.3
  5.7 0.0 copy-start.4
  5.7 0.0 copy-start.5
  5.7 0.0 copy-start.6
  5.8 1.1 copy.19
  6.8 6.9 %all-to-all-done.q_ref = bf16[4,4,72,256]{3,2,1,0:T(8,128)(2,1)S(1)} async-done(((bf16[4,4,72,256]{3,2,1,0:T(8,128)(2,1)}), bf16[4,4,72,256]{3,2,1,0:T(8,128)(2,1)S(1)}, u32[]{:S(2)}, u32[]{:S(2)}) %all-to-all-start) | async-done | bytes 589856 | tf_op jit(solution)/shard_map/all_to_all | solution.py:54
  13.8 3.5 %all-to-all-start.1 = ((bf16[4,4,72,256]{3,2,1,0:T(8,128)(2,1)}), bf16[4,4,72,256]{3,2,1,0:T(8,128)(2,1)S(1)}, u32[]{:S(2)}, u32[]{:S(2)}) async-start(bf16[4,4,72,256]{3,2,1,0:T(8,128)(2,1)} %bitcast.5), calls=%async_computation.1 | async-start | bytes 1179648 | tf_op jit(solution)/shard_map/all_to_all | solution.py:54
  17.2 1.1 copy.20
  18.3 6.3 %all-to-all-done.1.k_ref = bf16[4,4,72,256]{3,2,1,0:T(8,128)(2,1)S(1)} async-done(((bf16[4,4,72,256]{3,2,1,0:T(8,128)(2,1)}), bf16[4,4,72,256]{3,2,1,0:T(8,128)(2,1)S(1)}, u32[]{:S(2)}, u32[]{:S(2)}) %all-to-all-start.1) | async-done | bytes 589856 | tf_op jit(solution)/shard_map/all_to_all | solution.py:54
  24.6 3.5 %all-to-all-start.2 = ((bf16[4,4,72,256]{3,2,1,0:T(8,128)(2,1)}), bf16[4,4,72,256]{3,2,1,0:T(8,128)(2,1)S(1)}, u32[]{:S(2)}, u32[]{:S(2)}) async-start(bf16[4,4,72,256]{3,2,1,0:T(8,128)(2,1)} %bitcast.8), calls=%async_computation.2 | async-start | bytes 1179648 | tf_op jit(solution)/shard_map/all_to_all | solution.py:54
  28.1 0.6 broadcast_in_dim.20.out_bias_ref
  28.7 0.0 copy-done.4
  28.7 0.7 reshape.63.reduce_bias_ref
  29.4 0.2 copy.21
  29.6 0.8 fusion.where_ref
  30.5 4.2 %all-to-all-done.2.v_ref = bf16[4,4,72,256]{3,2,1,0:T(8,128)(2,1)S(1)} async-done(((bf16[4,4,72,256]{3,2,1,0:T(8,128)(2,1)}), bf16[4,4,72,256]{3,2,1,0:T(8,128)(2,1)S(1)}, u32[]{:S(2)}, u32[]{:S(2)}) %all-to-all-start.2) | async-done | bytes 589856 | tf_op jit(solution)/shard_map/all_to_all | solution.py:54
  34.7 12.4 %shard_map.136 = bf16[4,4,72,256]{3,2,1,0:T(8,128)(2,1)S(1)} custom-call(bf16[4,4,72,256]{3,2,1,0:T(8,128)(2,1)S(1)} %all-to-all-done.q_ref, bf16[4,4,72,256]{3,2,1,0:T(8,128)(2,1)S(1)} %all-to-all-done.1.k_ref, bf16[4,4,72,256]{3,2,1,0:T(8,128)(2,1)S(1)} %all-to-all-done.2.v_ref), custom_call_target="tpu_custom_call" | custom-call | tf_op jit(solution)/shard_map/pallas_call | solution.py:43
  47.1 0.0 copy-start
  47.1 0.8 copy-done
  47.9 0.7 broadcast_in_dim.22.counts_ref
  48.6 91.6 %shard_map.137 = bf16[256,1152]{1,0:T(8,128)(2,1)} custom-call(bf16[4,288,256]{2,1,0:T(8,128)(2,1)} %bitcast.21, bf16[256,1152]{1,0:T(8,128)(2,1)} %bitcast.25, f32[4,1152]{1,0:T(4,128)} %bitcast.29, f32[1,1152]{1,0:T(1,128)} %broadcast_in_dim.20.out_bias_ref, bf16[8,1152]{1,0:T(8,128)(2,1)} %bitcast.30, f32[1,1152]{1,0:T(1,128)} %expand_bias_ref.1, ...), custom_call_target="tpu_custom_call" | custom-call | tf_op jit(solution)/shard_map/pallas_call | solution.py:291
  140.2 1.9 %copy.23 = bf16[1,256,1152]{2,1,0:T(8,128)(2,1)} copy(bf16[1,256,1152]{2,1,0:T(8,128)(2,1)} %bitcast.24) | data formatting | bytes 1179648
  (8 shorter events, 0.0 us)
Async XLA Ops:
  0.0 5.8 %copy-start.1 = (bf16[1,256,1152]{2,1,0:T(8,128)(2,1)S(1)}, bf16[1,256,1152]{2,1,0:T(8,128)(2,1)}, u32[]{:S(2)}) copy-start(bf16[1,256,1152]{2,1,0:T(8,128)(2,1)} %param.16) | copy-start | bytes 1769476
  0.0 17.2 %copy-start.2 = (bf16[1,256,1152]{2,1,0:T(8,128)(2,1)S(1)}, bf16[1,256,1152]{2,1,0:T(8,128)(2,1)}, u32[]{:S(2)}) copy-start(bf16[1,256,1152]{2,1,0:T(8,128)(2,1)} %param.17) | copy-start | bytes 1769476
  2.2 11.5 %all-to-all-start = ((bf16[4,4,72,256]{3,2,1,0:T(8,128)(2,1)}), bf16[4,4,72,256]{3,2,1,0:T(8,128)(2,1)S(1)}, u32[]{:S(2)}, u32[]{:S(2)}) async-start(bf16[4,4,72,256]{3,2,1,0:T(8,128)(2,1)} %bitcast.2), calls=%async_computation | async-start | bytes 1179648 | tf_op jit(solution)/shard_map/all_to_all | solution.py:54
  5.7 22.4 %copy-start.3 = (f32[1152]{0:T(1024)S(1)}, f32[1152]{0:T(1024)}, u32[]{:S(2)}) copy-start(f32[1152]{0:T(1024)} %param.20) | copy-start | bytes 13828
  5.7 23.0 %copy-start.4 = (f32[1,1152]{1,0:T(1,128)S(1)}, f32[1,1152]{1,0:T(1,128)}, u32[]{:S(2)}) copy-start(f32[1,1152]{1,0:T(1,128)} %param.25) | copy-start | bytes 13828
  5.7 23.7 %copy-start.5 = (s32[8,1,96]{2,1,0:T(1,128)S(1)}, s32[8,1,96]{2,1,0:T(1,128)}, u32[]{:S(2)}) copy-start(s32[8,1,96]{2,1,0:T(1,128)} %param.27) | copy-start | bytes 9220
  5.7 23.9 %copy-start.6 = (s32[8,1]{0,1:T(1,128)S(1)}, s32[8,1]{0,1:T(1,128)}, u32[]{:S(2)}) copy-start(s32[8,1]{0,1:T(1,128)} %param.26) | copy-start | bytes 100
  13.8 10.9 %all-to-all-start.1 = ((bf16[4,4,72,256]{3,2,1,0:T(8,128)(2,1)}), bf16[4,4,72,256]{3,2,1,0:T(8,128)(2,1)S(1)}, u32[]{:S(2)}, u32[]{:S(2)}) async-start(bf16[4,4,72,256]{3,2,1,0:T(8,128)(2,1)} %bitcast.5), calls=%async_computation.1 | async-start | bytes 1179648 | tf_op jit(solution)/shard_map/all_to_all | solution.py:54
  24.6 10.1 %all-to-all-start.2 = ((bf16[4,4,72,256]{3,2,1,0:T(8,128)(2,1)}), bf16[4,4,72,256]{3,2,1,0:T(8,128)(2,1)S(1)}, u32[]{:S(2)}, u32[]{:S(2)}) async-start(bf16[4,4,72,256]{3,2,1,0:T(8,128)(2,1)} %bitcast.8), calls=%async_computation.2 | async-start | bytes 1179648 | tf_op jit(solution)/shard_map/all_to_all | solution.py:54
  47.1 0.8 copy-start

commit v3 on v2

v3 whole, which is shorter than its diff:
```python
import math

import jax
import jax.numpy as jnp
from jax import lax
from jax.experimental import pallas as pl
from jax.experimental.pallas import tpu as pltpu
from jax.sharding import PartitionSpec as P

H = 16
HD = 72
CAP = 256
BF = jnp.bfloat16
F32 = jnp.float32


def dot(a, b, ca, cb):
    return lax.dot_general(a, b, (((ca,), (cb,)), ((), ())), preferred_element_type=F32)


MESH = pl.DeviceIdType.MESH


def gelu(x):
    return 0.5 * x * (1.0 + jnp.tanh(math.sqrt(2.0 / math.pi) * (x + 0.044715 * (x * x * x))))


def layer_kernel(
    q_ref,
    k_ref,
    v_ref,
    stream_ref,
    mod_ref,
    out_bias_ref,
    router_ref,
    expand_bias_ref,
    reduce_bias_ref,
    counts_ref,
    where_ref,
    wo_hbm,
    we_hbm,
    wr_hbm,
    o_ref,
    wo,
    we,
    wr,
    qkv_out,
    qkv_in,
    att_out,
    att_in,
    picks,
    packs,
    packs_turned,
    normed_out,
    normed_in,
    gate_out,
    gate_in,
    count_in,
    chosen_out,
    chosen_in,
    rows_all,
    part_out,
    part_in,
    ret_out,
    ret_in,
    mix_out,
    mix_in,
    local_sem,
    head_send,
    head_recv,
    tok_send,
    tok_recv,
    frame_send,
    frame_recv,
):
    shards, heads, _, tokens = att_in.shape
    cols = heads * HD
    frames, slots = chosen_in.shape[0], chosen_in.shape[1]
    experts = gate_in.shape[1]
    frame_tokens = shards * tokens
    size = {"tok": shards, "frame": frames}
    me = {"tok": lax.axis_index("tok"), "frame": lax.axis_index("frame")}
    sems = {
        "tok": (tok_send, tok_recv),
        "frame": (frame_send, frame_recv),
        "head": (head_send, head_recv),
    }
    size["head"], me["head"] = size["tok"], me["tok"]
    real = {"tok": "tok", "frame": "frame", "head": "tok"}

    loads = [
        pltpu.make_async_copy(src, dst, local_sem.at[i])
        for i, (src, dst) in enumerate(((wo_hbm, wo), (we_hbm, we), (wr_hbm, wr)))
    ]
    for load in loads:
        load.start()

    barrier = pltpu.get_barrier_semaphore()
    for axis in ("tok", "frame"):
        for d in range(1, size[axis]):
            p = lax.rem(me[axis] + d, size[axis])
            pl.semaphore_signal(barrier, inc=1, device_id={axis: p}, device_id_type=MESH)
    pl.semaphore_wait(barrier, shards + frames - 2)

    def copy(axis, phase, src, dst, to, slot):
        send, recv = sems[axis]
        return pltpu.make_async_remote_copy(
            src_ref=src,
            dst_ref=dst.at[slot],
            send_sem=send.at[phase, to],
            recv_sem=recv.at[phase, slot],
            device_id={real[axis]: to},
            device_id_type=MESH,
        )

    sent = []

    def send_to(axis, phase, source, dst, d):
        p = lax.rem(me[axis] + d, size[axis])
        made = copy(axis, phase, source(p), dst, p, me[axis])
        made.start()
        sent.append(made)

    def send_all(axis, phase, source, dst):
        for d in range(1, size[axis]):
            send_to(axis, phase, source, dst, d)

    def take(axis, phase, source, dst, d):
        q = lax.rem(me[axis] + size[axis] - d, size[axis])
        copy(axis, phase, source(q), dst, q, q).wait_recv()
        return q

    def take_all(axis, phase, source, dst):
        for d in range(1, size[axis]):
            take(axis, phase, source, dst, d)

    tok, frame = me["tok"], me["frame"]
    send_all("frame", 0, lambda p: counts_ref.at[p], count_in)
    count_in[frame] = counts_ref[frame]

    def part(t, h):
        return (t * heads + h, lambda p: qkv_out.at[t, p, h], qkv_in.at[t, :, h])

    for t, ref in enumerate((k_ref, q_ref, v_ref)):
        turned = ref[...].astype(F32).T
        for h in range(heads):
            for s in range(shards):
                base = s * cols + h * HD
                qkv_out[t, s, h] = turned[base : base + HD].astype(BF)
            if h == 0:
                send_all("head", *part(t, h))
    for h in range(1, heads):
        for t in range(3):
            send_all("head", *part(t, h))
    for t in range(3):
        qkv_in[t, tok] = qkv_out[t, tok]

    token = lax.broadcasted_iota(jnp.int32, (slots, frame_tokens), 1)
    for e in range(experts):
        picks[e] = jnp.where(where_ref[e] == token, 1.0, 0.0).astype(BF)

    scale = math.log2(math.e) / math.sqrt(HD)
    for h in range(heads):
        for t in range(3):
            take_all("head", *part(t, h))
        keys = jnp.concatenate([qkv_in[0, s, h] for s in range(shards)], axis=1).T
        values = jnp.concatenate([qkv_in[2, s, h] for s in range(shards)], axis=1)

        def block(j, carry):
            scores = dot(keys, qkv_in[1, j, h], 1, 0)
            top = jnp.max(scores, axis=0, keepdims=True)
            powers = jnp.exp2((scores - top) * scale)
            denominator = jnp.sum(powers, axis=0, keepdims=True)
            out = dot(values, powers.astype(BF), 1, 0)
            att_out[j, h] = (out / denominator).astype(BF)
            return carry

        lax.fori_loop(0, shards, block, 0)
        send_all("head", 3 * heads + h, lambda p: att_out.at[p, h], att_in.at[:, h])
        att_in[tok, h] = att_out[tok, h]

    take_all("frame", 0, lambda p: counts_ref.at[p], count_in)
    row = lax.broadcasted_iota(jnp.int32, (CAP, slots), 0)
    slot = lax.broadcasted_iota(jnp.int32, (CAP, slots), 1)
    first = jnp.zeros((1, slots), jnp.int32)
    for g in range(frames):
        number = count_in[g][0:1, 0:slots]
        pack = jnp.where((row == first + slot) & (slot < number), 1.0, 0.0)
        packs[g] = pack.astype(BF)
        packs_turned[g] = pack.T.astype(BF)
        first = first + number
    loads[0].wait()

    def project(q):
        block = jnp.concatenate([att_in[q, h].astype(F32) for h in range(heads)], axis=0)
        return dot(block.T.astype(BF), wo[q], 1, 0)

    projected = project(tok)
    for d in range(1, shards):
        for h in range(heads):
            q = take("head", 3 * heads + h, lambda p: att_out.at[p, h], att_in.at[:, h], d)
        projected += project(q)
    projected += out_bias_ref[...]
    residual = (stream_ref[...].astype(F32) + mod_ref[0:1] * projected).astype(BF)
    wide = residual.astype(F32)
    centred = wide - jnp.mean(wide, axis=1, keepdims=True)
    variance = jnp.mean(centred * centred, axis=1, keepdims=True)
    normed = (
        centred * lax.rsqrt(variance + 1e-06) * (1.0 + mod_ref[2:3]) + mod_ref[1:2]
    ).astype(BF)
    turned = normed.T
    for s in range(shards):
        normed_out[s] = turned[s * cols : (s + 1) * cols]
    send_all("tok", 1, lambda p: normed_out.at[p], normed_in)
    o_ref[...] = residual
    gates = dot(router_ref[...], normed, 1, 1)
    gate_out[...] = 1.0 / (1.0 + jnp.exp(-gates))
    send_all("tok", 2, lambda p: gate_out, gate_in)
    normed_in[tok] = normed_out[tok]
    gate_in[tok] = gate_out[...]

    take_all("tok", 1, lambda p: normed_out.at[p], normed_in)
    held = jnp.concatenate([normed_in[s] for s in range(shards)], axis=1)
    for d in range(1, frames + 1):
        p = lax.rem(frame + d, frames)
        chosen_out[p] = dot(picks[p], held, 1, 1).astype(BF)
        if d < frames:
            send_to("frame", 1, lambda p: chosen_out.at[p], chosen_in, d)
    rows = dot(packs[frame], chosen_out[frame], 1, 0)
    for d in range(1, frames):
        g = take("frame", 1, lambda p: chosen_out.at[p], chosen_in, d)
        rows += dot(packs[g], chosen_in[g], 1, 0)
    rows_all[tok] = rows.astype(BF)
    send_all("tok", 3, lambda p: rows_all.at[tok], rows_all)
    loads[1].wait()
    loads[2].wait()
    hidden = dot(rows_all[tok], we[tok], 1, 0)
    for d in range(1, shards):
        q = take("tok", 3, lambda p: rows_all.at[tok], rows_all, d)
        hidden += dot(rows_all[q], we[q], 1, 0)
    hidden = gelu(hidden + expand_bias_ref[...]).astype(BF)
    partial_out = dot(hidden, wr[...], 1, 0)
    for s in range(shards):
        part_out[s] = partial_out[:, s * cols : (s + 1) * cols].astype(BF)
    send_all("tok", 4, lambda p: part_out.at[p], part_in)
    part_in[tok] = part_out[tok]
    take_all("tok", 4, lambda p: part_out.at[p], part_in)
    total = part_in[0].astype(F32)
    for s in range(1, shards):
        total += part_in[s].astype(F32)
    expert_out = (total + reduce_bias_ref[tok]).astype(BF)
    for d in range(1, frames + 1):
        p = lax.rem(frame + d, frames)
        ret_out[p] = dot(packs_turned[p], expert_out, 1, 0).astype(BF)
        if d < frames:
            send_to("frame", 2, lambda p: ret_out.at[p], ret_in, d)
    take_all("tok", 2, lambda p: gate_out, gate_in)
    gate_all = jnp.concatenate([gate_in[s] for s in range(shards)], axis=1).astype(BF)
    for e in range(experts):
        picks[e] = picks[e] * gate_all[e : e + 1]
    mixed = dot(ret_out[frame].T, picks[frame], 1, 0)
    for d in range(1, frames):
        e = take("frame", 2, lambda p: ret_out.at[p], ret_in, d)
        mixed += dot(ret_in[e].T, picks[e], 1, 0)
    for s in range(shards):
        mix_out[s] = mixed[:, s * tokens : (s + 1) * tokens].astype(BF)
    send_all("tok", 5, lambda p: mix_out.at[p], mix_in)
    mix_in[tok] = mix_out[tok]
    take_all("tok", 5, lambda p: mix_out.at[p], mix_in)
    mix = jnp.concatenate([mix_in[s].astype(F32) for s in range(shards)], axis=0).T
    o_ref[...] = (o_ref[...].astype(F32) + mod_ref[3:4] * mix).astype(BF)
    for made in sent:
        made.wait_send()


def per_device(
    stream,
    queries,
    key_vectors,
    value_vectors,
    modulation,
    output_weight,
    output_bias,
    router_weight,
    expand_weight,
    expand_bias,
    reduce_weight,
    reduce_bias,
    counts,
    picked_rows,
):
    shards = lax.axis_size("tok")
    frames = lax.axis_size("frame")
    tokens = stream.shape[1]
    width = stream.shape[2]
    hidden = expand_weight.shape[2]
    cols = width // shards
    heads = H // shards
    experts, _, slots = picked_rows.shape

    used = jnp.arange(slots, dtype=jnp.int32)[None, :] < counts
    where_to = jnp.where(used, picked_rows[:, 0, :], -1)[:, :, None]
    vmem = pl.BlockSpec(memory_space=pltpu.VMEM)
    hbm = pl.BlockSpec(memory_space=pl.ANY)
    layer_out = pl.pallas_call(
        layer_kernel,
        out_shape=jax.ShapeDtypeStruct((tokens, width), BF),
        in_specs=[vmem] * 11 + [hbm] * 3,
        out_specs=vmem,
        scratch_shapes=[
            pltpu.VMEM((shards, cols, width), BF),
            pltpu.VMEM((shards, cols, hidden), BF),
            pltpu.VMEM((hidden, width), BF),
            pltpu.VMEM((3, shards, heads, HD, tokens), BF),
            pltpu.VMEM((3, shards, heads, HD, tokens), BF),
            pltpu.VMEM((shards, heads, HD, tokens), BF),
            pltpu.VMEM((shards, heads, HD, tokens), BF),
            pltpu.VMEM((experts, slots, shards * tokens), BF),
            pltpu.VMEM((frames, CAP, slots), BF),
            pltpu.VMEM((frames, slots, CAP), BF),
            pltpu.VMEM((shards, cols, tokens), BF),
            pltpu.VMEM((shards, cols, tokens), BF),
            pltpu.VMEM((experts, tokens), F32),
            pltpu.VMEM((shards, experts, tokens), F32),
            pltpu.VMEM((frames, 8, 128), jnp.int32),
            pltpu.VMEM((frames, slots, cols), BF),
            pltpu.VMEM((frames, slots, cols), BF),
            pltpu.VMEM((shards, CAP, cols), BF),
            pltpu.VMEM((shards, CAP, cols), BF),
            pltpu.VMEM((shards, CAP, cols), BF),
            pltpu.VMEM((frames, slots, cols), BF),
            pltpu.VMEM((frames, slots, cols), BF),
            pltpu.VMEM((shards, cols, tokens), BF),
            pltpu.VMEM((shards, cols, tokens), BF),
            pltpu.SemaphoreType.DMA((3,)),
            pltpu.SemaphoreType.DMA((4 * heads, shards)),
            pltpu.SemaphoreType.DMA((4 * heads, shards)),
            pltpu.SemaphoreType.DMA((6, shards)),
            pltpu.SemaphoreType.DMA((6, shards)),
            pltpu.SemaphoreType.DMA((3, frames)),
            pltpu.SemaphoreType.DMA((3, frames)),
        ],
        compiler_params=pltpu.CompilerParams(
            collective_id=1, has_side_effects=True, vmem_limit_bytes=56 << 20
        ),
    )(
        queries[0],
        key_vectors[0],
        value_vectors[0],
        stream[0],
        modulation[0],
        output_bias[None],
        router_weight.T,
        expand_bias,
        reduce_bias.reshape(shards, 1, cols),
        jnp.broadcast_to(counts[:, :, None], (experts, 8, 128)),
        where_to,
        output_weight.reshape(shards, cols, width),
        expand_weight[0].reshape(shards, cols, hidden),
        reduce_weight[0],
    )
    return layer_out[None]


def solution(mesh):
    return jax.shard_map(
        per_device,
        mesh=mesh,
        in_specs=(
            P("frame", "tok", None),
            P("frame", "tok", None),
            P("frame", "tok", None),
            P("frame", "tok", None),
            P("frame", None, None),
            P(),
            P(),
            P(),
            P("frame", None, "tok"),
            P("frame", "tok"),
            P("frame", "tok", None),
            P("frame", None),
            P(None, "frame"),
            P(None, "frame", None),
        ),
        out_specs=P("frame", "tok", None),
        check_vma=False,
    )
```

time: 143 us -> 112 us (0.78)
  waiting for transfers between devices: 17.5 us -> 0 us
  starting transfers between devices: 10.4 us -> 0 us
  local copies, waits for them, and re-layouts: 9.25 us -> 6.08 us
    all_to_all x3 -> x0, waiting for transfers between devices: 17.5 us -> none  [swap(): return lax.all_to_all(x, axis, split_axis=0, concat_axis=0, tiled=True)]
    all_to_all x3 -> x0, starting transfers between devices: 10.4 us -> none  [swap(): return lax.all_to_all(x, axis, split_axis=0, concat_axis=0, tiled=True)]
    transpose x3 -> x0, local copies, waits for them, and re-layouts: 4.34 us -> none  [to_heads(): return swap(x[0].T.reshape(shards, heads, HD, tokens), 'tok')]
    pallas_call x2 -> x1, Pallas kernels: 104 us -> 104 us  [per_device(): pl.pallas_call(layer_kernel, out_shape=jax.ShapeDtypeStruct((tokens, widt...]
  transfers between devices with their start and end apart: 3 -> 0, of which waited for: 3 -> 0; matrix products, arithmetic and copies ran while one was open for 3% -> 0% of each run, Pallas kernels for 0% -> 0%
where the time goes in v3:
time: 112 us
  Pallas kernels  104 us (93%)
  local copies, waits for them, and re-layouts  6.08 us (5%)
  other arithmetic  2.21 us (2%)
    pallas_call x1, Pallas kernels, per_device(): pl.pallas_call(layer_kernel, out_shape=jax.ShapeDtypeStruct((tokens, widt...  104 us

profile of v3, /device:TPU:25, one launch (start us, length us, event | category | flops | bytes accessed | tf_op | source)
XLA Modules:
  0.0 111.9 jit_solution(1484996685342622834)
XLA Ops:
  0.0 1.3 %broadcast_in_dim.20.out_bias_ref = f32[1,1152]{1,0:T(1,128)} reshape(f32[1152]{0:T(1024)} %param.20) | data formatting | bytes 9216 | tf_op jit(solution)/shard_map/broadcast_in_dim | solution.py:352
  1.3 0.7 reduce
  2.0 0.7 reshape.50.reduce_bias_ref
  2.7 1.3 %broadcast_in_dim.22.counts_ref = s32[8,8,128]{2,1,0:T(8,128)} broadcast(s32[8]{0:T(128)} %bitcast.23), dimensions={0} | broadcast | bytes 32800 | tf_op jit(solution)/shard_map/broadcast_in_dim | solution.py:356
  4.0 0.9 copy.15
  4.9 1.5 %fusion.where_ref = s32[8,96,1]{2,1,0:T(8,128)} fusion(s32[8,96,1]{2,1,0:T(8,128)S(1)} %copy.15, s32[8]{0:T(128)} %bitcast.24), kind=kLoop, calls=%fused_computation.1 | loop fusion | flops 1536 | bytes 6176 | tf_op jit(solution)/shard_map/jit(_where)/select_n | solution.py:302
  6.4 103.5 %shard_map.136 = bf16[256,1152]{1,0:T(8,128)(2,1)} custom-call(bf16[256,1152]{1,0:T(8,128)(2,1)} %bitcast.16, bf16[256,1152]{1,0:T(8,128)(2,1)} %bitcast.17, bf16[256,1152]{1,0:T(8,128)(2,1)} %bitcast.18, bf16[256,1152]{1,0:T(8,128)(2,1)} %bitcast.19, f32[4,1152]{1,0:T(4,128)} %bitcast.20, f32[1,1152]{1,0:T(1,128)} %broadcast_in_dim.20.out_bias_ref, ...), custom_call_target="tpu_custom_call" | custom-call | tf_op jit(solution)/shard_map/pallas_call | solution.py:305
  109.9 1.9 %copy.17 = bf16[1,256,1152]{2,1,0:T(8,128)(2,1)} copy(bf16[1,256,1152]{2,1,0:T(8,128)(2,1)} %bitcast.15) | data formatting | bytes 1179648

commit v4 on v3

--- a/solution.py
+++ b/solution.py
@@ -23,6 +23,38 @@
 
 def gelu(x):
     return 0.5 * x * (1.0 + jnp.tanh(math.sqrt(2.0 / math.pi) * (x + 0.044715 * (x * x * x))))
+
+
+def packed_shape(slots, cols):
+    full, rest = cols // 128, cols % 128
+    if full and rest and 128 % rest == 0 and slots % (128 // rest) == 0:
+        if slots * rest // 128 % 8 == 0 and slots % 16 == 0:
+            return (full * slots + slots * rest // 128, 128)
+    return (slots, cols)
+
+
+def put_block(ref, at, x, slots):
+    cols = x.shape[1]
+    if ref.shape[1:] == (slots, cols):
+        ref[at] = x.astype(BF)
+        return
+    full, rest = cols // 128, cols % 128
+    for i in range(full):
+        ref[at, i * slots : (i + 1) * slots, :] = x[:, i * 128 : (i + 1) * 128].astype(BF)
+    high = slots * rest // 128
+    tail = [x[i * high : (i + 1) * high, full * 128 :] for i in range(128 // rest)]
+    ref[at, full * slots : full * slots + high, :] = jnp.concatenate(tail, axis=1).astype(BF)
+
+
+def get_block(ref, at, slots, cols):
+    if ref.shape[1:] == (slots, cols):
+        return ref[at]
+    full, rest = cols // 128, cols % 128
+    high = slots * rest // 128
+    parts = [ref[at, i * slots : (i + 1) * slots, :] for i in range(full)]
+    tail = ref[at, full * slots : full * slots + high, :].astype(F32)
+    tail = [tail[:, i * rest : (i + 1) * rest] for i in range(128 // rest)]
+    return jnp.concatenate(parts + [jnp.concatenate(tail, axis=0).astype(BF)], axis=1)
 
 
 def layer_kernel(
@@ -75,7 +107,7 @@
 ):
     shards, heads, _, tokens = att_in.shape
     cols = heads * HD
-    frames, slots = chosen_in.shape[0], chosen_in.shape[1]
+    frames, slots = packs.shape[0], packs.shape[2]
     experts = gate_in.shape[1]
     frame_tokens = shards * tokens
     size = {"tok": shards, "frame": frames}
@@ -223,25 +255,25 @@
     held = jnp.concatenate([normed_in[s] for s in range(shards)], axis=1)
     for d in range(1, frames + 1):
         p = lax.rem(frame + d, frames)
-        chosen_out[p] = dot(picks[p], held, 1, 1).astype(BF)
+        put_block(chosen_out, p, dot(picks[p], held, 1, 1), slots)
         if d < frames:
             send_to("frame", 1, lambda p: chosen_out.at[p], chosen_in, d)
-    rows = dot(packs[frame], chosen_out[frame], 1, 0)
+    rows = dot(packs[frame], get_block(chosen_out, frame, slots, cols), 1, 0)
     for d in range(1, frames):
         g = take("frame", 1, lambda p: chosen_out.at[p], chosen_in, d)
-        rows += dot(packs[g], chosen_in[g], 1, 0)
-    rows_all[tok] = rows.astype(BF)
+        rows += dot(packs[g], get_block(chosen_in, g, slots, cols), 1, 0)
+    rows_all[tok] = rows.T.astype(BF)
     send_all("tok", 3, lambda p: rows_all.at[tok], rows_all)
     loads[1].wait()
     loads[2].wait()
-    hidden = dot(rows_all[tok], we[tok], 1, 0)
+    hidden = dot(rows_all[tok].T, we[tok], 1, 0)
     for d in range(1, shards):
         q = take("tok", 3, lambda p: rows_all.at[tok], rows_all, d)
-        hidden += dot(rows_all[q], we[q], 1, 0)
+        hidden += dot(rows_all[q].T, we[q], 1, 0)
     hidden = gelu(hidden + expand_bias_ref[...]).astype(BF)
-    partial_out = dot(hidden, wr[...], 1, 0)
+    partial_out = dot(hidden, wr[...], 1, 0).T
     for s in range(shards):
-        part_out[s] = partial_out[:, s * cols : (s + 1) * cols].astype(BF)
+        part_out[s] = partial_out[s * cols : (s + 1) * cols].astype(BF)
     send_all("tok", 4, lambda p: part_out.at[p], part_in)
     part_in[tok] = part_out[tok]
     take_all("tok", 4, lambda p: part_out.at[p], part_in)
@@ -251,17 +283,17 @@
     expert_out = (total + reduce_bias_ref[tok]).astype(BF)
     for d in range(1, frames + 1):
         p = lax.rem(frame + d, frames)
-        ret_out[p] = dot(packs_turned[p], expert_out, 1, 0).astype(BF)
+        put_block(ret_out, p, dot(packs_turned[p], expert_out, 1, 1), slots)
         if d < frames:
             send_to("frame", 2, lambda p: ret_out.at[p], ret_in, d)
     take_all("tok", 2, lambda p: gate_out, gate_in)
     gate_all = jnp.concatenate([gate_in[s] for s in range(shards)], axis=1).astype(BF)
     for e in range(experts):
         picks[e] = picks[e] * gate_all[e : e + 1]
-    mixed = dot(ret_out[frame].T, picks[frame], 1, 0)
+    mixed = dot(get_block(ret_out, frame, slots, cols).T, picks[frame], 1, 0)
     for d in range(1, frames):
         e = take("frame", 2, lambda p: ret_out.at[p], ret_in, d)
-        mixed += dot(ret_in[e].T, picks[e], 1, 0)
+        mixed += dot(get_block(ret_in, e, slots, cols).T, picks[e], 1, 0)
     for s in range(shards):
         mix_out[s] = mixed[:, s * tokens : (s + 1) * tokens].astype(BF)
     send_all("tok", 5, lambda p: mix_out.at[p], mix_in)
@@ -323,13 +355,13 @@
             pltpu.VMEM((experts, tokens), F32),
             pltpu.VMEM((shards, experts, tokens), F32),
             pltpu.VMEM((frames, 8, 128), jnp.int32),
-            pltpu.VMEM((frames, slots, cols), BF),
-            pltpu.VMEM((frames, slots, cols), BF),
-            pltpu.VMEM((shards, CAP, cols), BF),
-            pltpu.VMEM((shards, CAP, cols), BF),
-            pltpu.VMEM((shards, CAP, cols), BF),
-            pltpu.VMEM((frames, slots, cols), BF),
-            pltpu.VMEM((frames, slots, cols), BF),
+            pltpu.VMEM((frames, *packed_shape(slots, cols)), BF),
+            pltpu.VMEM((frames, *packed_shape(slots, cols)), BF),
+            pltpu.VMEM((shards, cols, CAP), BF),
+            pltpu.VMEM((shards, cols, CAP), BF),
+            pltpu.VMEM((shards, cols, CAP), BF),
+            pltpu.VMEM((frames, *packed_shape(slots, cols)), BF),
+            pltpu.VMEM((frames, *packed_shape(slots, cols)), BF),
             pltpu.VMEM((shards, cols, tokens), BF),
             pltpu.VMEM((shards, cols, tokens), BF),
             pltpu.SemaphoreType.DMA((3,)),
@@ -352,7 +384,7 @@
         output_bias[None],
         router_weight.T,
         expand_bias,
-        reduce_bias.reshape(shards, 1, cols),
+        reduce_bias.reshape(shards, cols, 1),
         jnp.broadcast_to(counts[:, :, None], (experts, 8, 128)),
         where_to,
         output_weight.reshape(shards, cols, width),

time: 112 us -> 103 us (0.920)
  Pallas kernels: 104 us -> 93.1 us
    pallas_call x1, Pallas kernels: 104 us -> 93.1 us  [per_device(): pl.pallas_call(layer_kernel, out_shape=jax.ShapeDtypeStruct((tokens, widt...]
where the time goes in v4:
time: 103 us; the launch traced here: 102 us
  Pallas kernels  93.1 us (90%)
  local copies, waits for them, and re-layouts  6.68 us (6%)
  other arithmetic  2.21 us (2%)
    pallas_call x1, Pallas kernels, per_device(): pl.pallas_call(layer_kernel, out_shape=jax.ShapeDtypeStruct((tokens, widt...  93.1 us

profile of v4, /device:TPU:25, one launch (start us, length us, event | category | flops | bytes accessed | tf_op | source)
XLA Modules:
  0.0 102.0 jit_solution(15421652335788124923)
XLA Ops:
  0.0 1.3 %broadcast_in_dim.20.out_bias_ref = f32[1,1152]{1,0:T(1,128)} reshape(f32[1152]{0:T(1024)} %param.20) | data formatting | bytes 9216 | tf_op jit(solution)/shard_map/broadcast_in_dim | solution.py:384
  1.3 0.7 reduce
  2.0 1.3 %broadcast_in_dim.22.counts_ref = s32[8,8,128]{2,1,0:T(8,128)} broadcast(s32[8]{0:T(128)} %bitcast.23), dimensions={0} | broadcast | bytes 32800 | tf_op jit(solution)/shard_map/broadcast_in_dim | solution.py:388
  3.4 0.9 copy.15
  4.2 1.5 %fusion.where_ref = s32[8,96,1]{2,1,0:T(8,128)} fusion(s32[8,96,1]{2,1,0:T(8,128)S(1)} %copy.15, s32[8]{0:T(128)} %bitcast.24), kind=kLoop, calls=%fused_computation.1 | loop fusion | flops 1536 | bytes 6176 | tf_op jit(solution)/shard_map/jit(_where)/select_n | solution.py:334
  5.7 1.3 %reshape.52.reduce_bias_ref = f32[4,288,1]{2,1,0:T(8,128)} reshape(f32[1152]{0:T(1024)S(1)} %reduce) | data formatting | bytes 9216 | tf_op jit(solution)/shard_map/reshape | solution.py:387
  7.0 93.1 %shard_map.136 = bf16[256,1152]{1,0:T(8,128)(2,1)} custom-call(bf16[256,1152]{1,0:T(8,128)(2,1)} %bitcast.16, bf16[256,1152]{1,0:T(8,128)(2,1)} %bitcast.17, bf16[256,1152]{1,0:T(8,128)(2,1)} %bitcast.18, bf16[256,1152]{1,0:T(8,128)(2,1)} %bitcast.19, f32[4,1152]{1,0:T(4,128)} %bitcast.20, f32[1,1152]{1,0:T(1,128)} %broadcast_in_dim.20.out_bias_ref, ...), custom_call_target="tpu_custom_call" | custom-call | tf_op jit(solution)/shard_map/pallas_call | solution.py:337
  100.1 1.9 %copy.18 = bf16[1,256,1152]{2,1,0:T(8,128)(2,1)} copy(bf16[1,256,1152]{2,1,0:T(8,128)(2,1)} %bitcast.15) | data formatting | bytes 1179648

commit v5 on v4

--- a/solution.py
+++ b/solution.py
@@ -66,9 +66,9 @@
     out_bias_ref,
     router_ref,
     expand_bias_ref,
-    reduce_bias_ref,
-    counts_ref,
-    where_ref,
+    reduce_bias_row,
+    own_counts_ref,
+    picked_ref,
     wo_hbm,
     we_hbm,
     wr_hbm,
@@ -87,6 +87,8 @@
     normed_in,
     gate_out,
     gate_in,
+    reduce_bias_ref,
+    counts_ref,
     count_in,
     chosen_out,
     chosen_in,
@@ -167,6 +169,8 @@
             take(axis, phase, source, dst, d)
 
     tok, frame = me["tok"], me["frame"]
+    for e in range(experts):
+        counts_ref[e] = jnp.broadcast_to(own_counts_ref[e : e + 1, :], (8, 128))
     send_all("frame", 0, lambda p: counts_ref.at[p], count_in)
     count_in[frame] = counts_ref[frame]
 
@@ -189,7 +193,13 @@
 
     token = lax.broadcasted_iota(jnp.int32, (slots, frame_tokens), 1)
     for e in range(experts):
-        picks[e] = jnp.where(where_ref[e] == token, 1.0, 0.0).astype(BF)
+        used = lax.broadcasted_iota(jnp.int32, (1, slots), 1) < counts_ref[e][0:1, 0:slots]
+        spot = jnp.where(used, picked_ref[e], -1).astype(F32)
+        column = jnp.broadcast_to(spot, (128, slots)).T[:, 0:1].astype(jnp.int32)
+        picks[e] = jnp.where(column == token, 1.0, 0.0).astype(BF)
+    bias_columns = jnp.broadcast_to(reduce_bias_row[...], (8, shards * cols)).T
+    for s in range(shards):
+        reduce_bias_ref[s] = bias_columns[s * cols : (s + 1) * cols, 0:1]
 
     scale = math.log2(math.e) / math.sqrt(HD)
     for h in range(heads):
@@ -232,7 +242,7 @@
         for h in range(heads):
             q = take("head", 3 * heads + h, lambda p: att_out.at[p, h], att_in.at[:, h], d)
         projected += project(q)
-    projected += out_bias_ref[...]
+    projected += out_bias_ref[...].reshape(1, shards * cols)
     residual = (stream_ref[...].astype(F32) + mod_ref[0:1] * projected).astype(BF)
     wide = residual.astype(F32)
     centred = wide - jnp.mean(wide, axis=1, keepdims=True)
@@ -330,8 +340,6 @@
     heads = H // shards
     experts, _, slots = picked_rows.shape
 
-    used = jnp.arange(slots, dtype=jnp.int32)[None, :] < counts
-    where_to = jnp.where(used, picked_rows[:, 0, :], -1)[:, :, None]
     vmem = pl.BlockSpec(memory_space=pltpu.VMEM)
     hbm = pl.BlockSpec(memory_space=pl.ANY)
     layer_out = pl.pallas_call(
@@ -354,6 +362,8 @@
             pltpu.VMEM((shards, cols, tokens), BF),
             pltpu.VMEM((experts, tokens), F32),
             pltpu.VMEM((shards, experts, tokens), F32),
+            pltpu.VMEM((shards, cols, 1), F32),
+            pltpu.VMEM((frames, 8, 128), jnp.int32),
             pltpu.VMEM((frames, 8, 128), jnp.int32),
             pltpu.VMEM((frames, *packed_shape(slots, cols)), BF),
             pltpu.VMEM((frames, *packed_shape(slots, cols)), BF),
@@ -381,12 +391,12 @@
         value_vectors[0],
         stream[0],
         modulation[0],
-        output_bias[None],
+        output_bias,
         router_weight.T,
         expand_bias,
-        reduce_bias.reshape(shards, cols, 1),
-        jnp.broadcast_to(counts[:, :, None], (experts, 8, 128)),
-        where_to,
+        reduce_bias,
+        counts,
+        picked_rows,
         output_weight.reshape(shards, cols, width),
         expand_weight[0].reshape(shards, cols, hidden),
         reduce_weight[0],

time: 103 us -> 96.9 us (0.941)
  local copies, waits for them, and re-layouts: 6.68 us -> 3.24 us
  other arithmetic: 2.21 us -> 0 us
    broadcast_in_dim x2 -> x0, local copies, waits for them, and re-layouts: 2.64 us -> none  [the longest x1 1.35 us: per_device(): jnp.broadcast_to(counts[:, :, None], (experts, 8, 128))]
    select_n x1 -> x0, other arithmetic: 1.5 us -> none  [per_device(): where_to = jnp.where(used, picked_rows[:, 0, :], -1)[:, :, None]]
    unnamed x1 -> x2, local copies, waits for them, and re-layouts: 1.92 us -> 3.24 us
    reshape x1 -> x0, local copies, waits for them, and re-layouts: 1.25 us -> none  [per_device(): reduce_bias.reshape(shards, cols, 1)]
where the time goes in v5:
time: 96.9 us; the launch traced here: 96.1 us
  Pallas kernels  92.9 us (96%)
  local copies, waits for them, and re-layouts  3.24 us (3%)
    pallas_call x1, Pallas kernels, per_device(): pl.pallas_call(layer_kernel, out_shape=jax.ShapeDtypeStruct((tokens, widt...  92.9 us
    unnamed x2, local copies, waits for them, and re-layouts  3.24 us

profile of v5, /device:TPU:25, one launch (start us, length us, event | category | flops | bytes accessed | tf_op | source)
XLA Modules:
  0.0 96.1 jit_solution(11591478082246684720)
XLA Ops:
  0.0 1.3 %copy.15.own_counts_ref = s32[8,1]{1,0:T(8,128)} copy(s32[8,1]{0,1:T(1,128)} %param.26) | data formatting | bytes 64 | tf_op args[12]
  1.3 92.9 %shard_map.136 = bf16[256,1152]{1,0:T(8,128)(2,1)} custom-call(bf16[256,1152]{1,0:T(8,128)(2,1)} %bitcast.14, bf16[256,1152]{1,0:T(8,128)(2,1)} %bitcast.15, bf16[256,1152]{1,0:T(8,128)(2,1)} %bitcast.16, bf16[256,1152]{1,0:T(8,128)(2,1)} %bitcast.17, f32[4,1152]{1,0:T(4,128)} %bitcast.18, f32[1152]{0:T(1024)} %out_bias_ref.1, bf16[8,1152]{1,0:T(8,128)(2,1)} %bitcast.19, ...), custom_call_target="tpu_custom_call" | custom-call | tf_op jit(solution)/shard_map/pallas_call | solution.py:345
  94.2 1.9 %copy.17 = bf16[1,256,1152]{2,1,0:T(8,128)(2,1)} copy(bf16[1,256,1152]{2,1,0:T(8,128)(2,1)} %bitcast.13) | data formatting | bytes 1179648
